TPU v7x, 512 devices: a whole 4x8x8 slice. The times are simulated.
512 devices in a mesh: tok: 8 (over z), wid: 64 (over x, y, core).
Axes of the slice: x: 4, y: 8, z: 8, core: 2. Of those that a mesh axis runs over, the one named last changes fastest.
Arguments:
- tokens: bfloat16 [1536, 4096], P('tok', 'wid'), may hold values from -80 to 80
- gate_a: bfloat16 [16384, 4096], P('wid', 'tok'), may hold values from -0.09375 to 0.09375
- up_a: bfloat16 [16384, 4096], P('wid', 'tok'), may hold values from -0.09375 to 0.09375
- gate_b: bfloat16 [16384, 4096], P('wid', 'tok'), may hold values from -0.09375 to 0.09375
- up_b: bfloat16 [16384, 4096], P('wid', 'tok'), may hold values from -0.09375 to 0.09375
- down_a: bfloat16 [16384, 4096], P('wid', 'tok'), may hold values from -0.125 to 0.125
- down_b: bfloat16 [16384, 4096], P('wid', 'tok'), may hold values from -0.125 to 0.125
- block_perm: int32 [128], replicated, may hold values from 0 to 127, each once
Outputs:
- merged: bfloat16 [1536, 4096], P('tok', 'wid')
Inputs may be any that keep to these rules, and one draw needn't show every extreme that they name: block_perm names every block number once.
All inputs are finite; a program needn't handle non-finite values.
Results may differ from a plain program's by a relative error of at most 0.0058.
Values may be sent and summed in bfloat16 or wider, within the bound.
A program may use at most 64 MiB of HBM per device.

v0:
```python
import jax
import jax.numpy as jnp
from jax import lax
from jax.sharding import PartitionSpec as P

FF = 16384
BLOCK = 128


def sigmoid_linear(preact):
    return preact / (1.0 + jnp.exp(-preact))


def reorder_blocks(matrix_in, block_perm):
    shaped = matrix_in.reshape(FF // BLOCK, BLOCK, matrix_in.shape[1])
    return jnp.take(shaped, block_perm, axis=0).reshape(matrix_in.shape)


def add_products(pieces, gathered):
    return tuple(
        (
            lax.dot_general(
                gathered, piece, (((1,), (1,)), ((), ())), preferred_element_type=jnp.float32
            )
            for piece in pieces
        )
    )


def local(tokens, gate_a, up_a, gate_b, up_b, down_a, down_b, block_perm):
    gathered = lax.all_gather(tokens, "wid", axis=1, tiled=True)
    row_count = gathered.shape[0]
    shipped = (
        lax.all_to_all(gate_b, "wid", split_axis=1, concat_axis=0, tiled=True),
        lax.all_to_all(up_b, "wid", split_axis=1, concat_axis=0, tiled=True),
        lax.all_to_all(down_b, "wid", split_axis=1, concat_axis=0, tiled=True),
    )
    gate_src, up_src, down_perm = (
        lax.all_to_all(
            reorder_blocks(shipped[0], block_perm), "wid", split_axis=0, concat_axis=1, tiled=True
        ),
        lax.all_to_all(
            reorder_blocks(shipped[1], block_perm), "wid", split_axis=0, concat_axis=1, tiled=True
        ),
        lax.all_to_all(
            reorder_blocks(shipped[2], block_perm), "wid", split_axis=0, concat_axis=1, tiled=True
        ),
    )
    gate_av, up_av, gate_bv, up_bv = add_products(
        (
            lax.all_gather(gate_a, "tok", axis=1, tiled=True),
            lax.all_gather(up_a, "tok", axis=1, tiled=True),
            lax.all_gather(gate_src, "tok", axis=1, tiled=True),
            lax.all_gather(up_src, "tok", axis=1, tiled=True),
        ),
        gathered,
    )
    hid_a = sigmoid_linear(gate_av) * up_av
    hid_b = sigmoid_linear(gate_bv) * up_bv
    hid_m = sigmoid_linear(0.5 * (gate_av + gate_bv)) * (0.5 * (up_av + up_bv))
    token_total = row_count * lax.axis_size("tok")
    totals = lax.psum(
        (jnp.sum(hid_a, axis=0), jnp.sum(hid_b, axis=0), jnp.sum(hid_m, axis=0)), "tok"
    )
    centers = tuple((total / token_total for total in totals))
    squares = lax.psum(
        (
            jnp.sum((hid_a - centers[0]) ** 2, axis=0),
            jnp.sum((hid_b - centers[1]) ** 2, axis=0),
            jnp.sum((hid_m - centers[2]) ** 2, axis=0),
        ),
        "tok",
    )
    spreads = tuple((square / token_total for square in squares))
    deviations = tuple((jnp.sqrt(spread + 1e-05) for spread in spreads))
    target_std = 0.5 * (deviations[0] + deviations[1])
    target_mean = 0.5 * (centers[0] + centers[1])
    repaired = ((hid_m - centers[2]) / deviations[2] * target_std + target_mean).astype(
        jnp.bfloat16
    )
    down_mid = ((down_a.astype(jnp.float32) + down_perm.astype(jnp.float32)) * 0.5).astype(
        jnp.bfloat16
    )
    partial_out = jnp.dot(
        repaired,
        lax.all_gather(down_mid, "tok", axis=1, tiled=True),
        preferred_element_type=jnp.float32,
    )
    summed = lax.psum_scatter(partial_out, "wid", scatter_dimension=1, tiled=True)
    return summed.astype(jnp.bfloat16)


def solution(mesh):
    return jax.shard_map(
        local,
        mesh=mesh,
        in_specs=(
            P("tok", "wid"),
            P("wid", "tok"),
            P("wid", "tok"),
            P("wid", "tok"),
            P("wid", "tok"),
            P("wid", "tok"),
            P("wid", "tok"),
            P(),
        ),
        out_specs=P("tok", "wid"),
        check_vma=False,
    )
```

profile of v0, /device:TPU:16, one launch (start us, length us, event | category | flops | bytes accessed | tf_op | source)
XLA Modules:
  0.0 485.1 jit_solution(15461387688074729571)
XLA Ops:
  6.5 0.0 copy-start.1
  6.5 0.0 copy-start.3
  6.5 0.0 all-gather.7.cloned.1.call-start
  6.5 0.7 all-gather.7.cloned.1.call-update
  7.3 0.0 all-gather.9.cloned.1.call-start
  7.3 0.7 all-gather.9.cloned.1.call-update
  8.0 0.0 all-gather.13.cloned.1.call-start
  8.1 0.7 all-gather.13.cloned.1.call-update
  8.7 1.8 copy.9
  10.5 10.5 %all-to-all-start = ((bf16[256,64,8]{0,2,1:T(8,128)(2,1)}), bf16[256,64,8]{0,2,1:T(8,128)(2,1)S(1)}, u32[]{:S(2)}, u32[]{:S(2)}) async-start(bf16[256,64,8]{0,2,1:T(8,128)(2,1)} %bitcast), calls=%async_computation | async-start | bytes 524288 | tf_op jit(solution)/shard_map/all_to_all | solution.py:34
  21.0 1.8 copy.10
  22.8 9.9 %all-to-all-done = bf16[256,64,8]{0,2,1:T(8,128)(2,1)S(1)} async-done(((bf16[256,64,8]{0,2,1:T(8,128)(2,1)}), bf16[256,64,8]{0,2,1:T(8,128)(2,1)S(1)}, u32[]{:S(2)}, u32[]{:S(2)}) %all-to-all-start) | async-done | bytes 262176 | tf_op jit(solution)/shard_map/all_to_all | solution.py:34
  32.7 6.3 %all-to-all-start.2 = ((bf16[256,64,8]{0,2,1:T(8,128)(2,1)}), bf16[256,64,8]{0,2,1:T(8,128)(2,1)S(1)}, u32[]{:S(2)}, u32[]{:S(2)}) async-start(bf16[256,64,8]{0,2,1:T(8,128)(2,1)} %bitcast.7), calls=%async_computation.2 | async-start | bytes 524288 | tf_op jit(solution)/shard_map/all_to_all | solution.py:35
  39.0 0.0 copy-done.1
  39.0 0.8 copy.12
  39.9 10.8 %all-to-all-done.2 = bf16[256,64,8]{0,2,1:T(8,128)(2,1)S(1)} async-done(((bf16[256,64,8]{0,2,1:T(8,128)(2,1)}), bf16[256,64,8]{0,2,1:T(8,128)(2,1)S(1)}, u32[]{:S(2)}, u32[]{:S(2)}) %all-to-all-start.2) | async-done | bytes 262176 | tf_op jit(solution)/shard_map/all_to_all | solution.py:35
  50.7 6.7 %all-to-all-start.4 = ((bf16[256,64,8]{0,2,1:T(8,128)(2,1)}), bf16[256,64,8]{0,2,1:T(8,128)(2,1)S(1)}, u32[]{:S(2)}, u32[]{:S(2)}) async-start(bf16[256,64,8]{0,2,1:T(8,128)(2,1)} %bitcast.14), calls=%async_computation.4 | async-start | bytes 524288 | tf_op jit(solution)/shard_map/all_to_all | solution.py:36
  57.4 0.0 all-gather.11.cloned.1.call-start
  57.5 0.0 copy-done.3
  57.5 0.7 gather_fusion
  58.2 0.7 gather_fusion.1
  58.9 10.2 %all-to-all-done.4 = bf16[256,64,8]{0,2,1:T(8,128)(2,1)S(1)} async-done(((bf16[256,64,8]{0,2,1:T(8,128)(2,1)}), bf16[256,64,8]{0,2,1:T(8,128)(2,1)S(1)}, u32[]{:S(2)}, u32[]{:S(2)}) %all-to-all-start.4) | async-done | bytes 262176 | tf_op jit(solution)/shard_map/all_to_all | solution.py:36
  69.1 0.7 gather_fusion.2
  69.8 0.0 copy-start.2
  69.8 0.9 broadcast_select_fusion.2
  70.8 19.0 %all_to_all.99 = bf16[64,256,8]{1,2,0:T(8,128)(2,1)} all-to-all(bf16[64,256,8]{1,2,0:T(8,128)(2,1)S(1)} %bitcast.48), channel_id=1, replica_groups=mesh['tok'=8,'wid'=64] {'wid'}, dimensions={0} | all-to-all | bytes 524288 | tf_op jit(solution)/shard_map/all_to_all | solution.py:39
  89.8 0.0 all-gather.11.cloned.1.call-update
  89.8 0.0 all-gather.15.cloned.1.call-start
  89.9 18.3 %all_to_all.100 = bf16[64,256,8]{1,2,0:T(8,128)(2,1)} all-to-all(bf16[64,256,8]{1,2,0:T(8,128)(2,1)S(1)} %bitcast.47), channel_id=1, replica_groups=mesh['tok'=8,'wid'=64] {'wid'}, dimensions={0} | all-to-all | bytes 524288 | tf_op jit(solution)/shard_map/all_to_all | solution.py:42
  108.2 0.0 all-gather.15.cloned.1.call-update
  108.2 6.3 %all-to-all-start.5 = ((bf16[64,256,8]{1,2,0:T(8,128)(2,1)}), bf16[64,256,8]{1,2,0:T(8,128)(2,1)S(1)}, u32[]{:S(2)}, u32[]{:S(2)}) async-start(bf16[64,256,8]{1,2,0:T(8,128)(2,1)} %bitcast.17), calls=%async_computation.5 | async-start | bytes 524288 | tf_op jit(solution)/shard_map/all_to_all | solution.py:45
  114.6 0.0 all-gather.17.cloned.1.call-start
  114.6 0.0 copy-done.2
  114.6 0.1 copy.11
  114.8 11.5 %all-to-all-done.5 = bf16[64,256,8]{1,2,0:T(8,128)(2,1)S(1)} async-done(((bf16[64,256,8]{1,2,0:T(8,128)(2,1)}), bf16[64,256,8]{1,2,0:T(8,128)(2,1)S(1)}, u32[]{:S(2)}, u32[]{:S(2)}) %all-to-all-start.5) | async-done | bytes 262176 | tf_op jit(solution)/shard_map/all_to_all | solution.py:45
  126.3 0.8 fusion.1
  127.1 0.0 all-gather.17.cloned.1.call-update
  127.1 0.0 reduce-scatter.2.cloned.1.call-start
  127.2 0.0 all-gather.7.cloned.1.call-done
  127.2 0.0 copy-start
  127.2 16.2 %all-gather.9.cloned.1.call-done = bf16[256,4096]{1,0:T(8,128)(2,1)} async-done(((bf16[256,512]{1,0:T(8,128)(2,1)}), bf16[256,4096]{1,0:T(8,128)(2,1)}) %all-gather.9.cloned.1.call-update) | async-done | bytes 2097168 | tf_op jit(solution)/shard_map/all_gather | solution.py:51
  143.4 3.1 fusion.10
  146.4 41.8 %all-gather.13.cloned.1.call-done = bf16[256,4096]{1,0:T(8,128)(2,1)} async-done(((bf16[256,512]{1,0:T(8,128)(2,1)}), bf16[256,4096]{1,0:T(8,128)(2,1)}) %all-gather.13.cloned.1.call-update) | async-done | bytes 2097168 | tf_op jit(solution)/shard_map/all_gather | solution.py:52
  188.2 0.0 copy-done
  188.2 2.4 fusion.11
  190.7 42.3 %all-gather.11.cloned.1.call-done = bf16[256,4096]{0,1:T(8,128)(2,1)} async-done(((bf16[256,512]{0,1:T(8,128)(2,1)}), bf16[256,4096]{0,1:T(8,128)(2,1)}) %all-gather.11.cloned.1.call-update) | async-done | bytes 2097168 | tf_op jit(solution)/shard_map/all_gather | solution.py:53
  232.9 2.4 convolution_bitcast_fusion.1
  235.4 42.2 %all-gather.15.cloned.1.call-done = bf16[256,4096]{0,1:T(8,128)(2,1)} async-done(((bf16[256,512]{0,1:T(8,128)(2,1)}), bf16[256,4096]{0,1:T(8,128)(2,1)}) %all-gather.15.cloned.1.call-update) | async-done | bytes 2097168 | tf_op jit(solution)/shard_map/all_gather | solution.py:54
  277.6 2.5 fusion.8
  280.1 15.7 %all-reduce.1 = (f32[256]{0:T(256)S(1)}, f32[256]{0:T(256)S(1)}, f32[256]{0:T(256)S(1)}) all-reduce(f32[256]{0:T(256)S(1)} %get-tuple-element.20, f32[256]{0:T(256)S(1)} %get-tuple-element.14, f32[256]{0:T(256)S(1)} %get-tuple-element.18), channel_id=1, replica_groups=mesh['tok'=8,'wid'=64] {'tok'}, use_global_device_ids=true, to_apply=%region_5.7 | all-reduce | flops 768 | bytes 6144 | tf_op jit(solution)/shard_map/psum | solution.py:62
  295.9 0.1 multiply_reduce_fusion
  295.9 14.7 %all-reduce = (f32[256]{0:T(256)S(1)}, f32[256]{0:T(256)S(1)}, f32[256]{0:T(256)S(1)}) all-reduce(f32[256]{0:T(256)S(1)} %get-tuple-element.28, f32[256]{0:T(256)S(1)} %get-tuple-element.29, f32[256]{0:T(256)S(1)} %multiply_reduce_fusion.2), channel_id=1, replica_groups=mesh['tok'=8,'wid'=64] {'tok'}, use_global_device_ids=true, to_apply=%region_11.13 | all-reduce | flops 768 | bytes 6144 | tf_op jit(solution)/shard_map/psum | solution.py:66
  310.7 11.2 %all-gather.17.cloned.1.call-done = bf16[256,4096]{0,1:T(8,128)(2,1)} async-done(((bf16[256,512]{0,1:T(8,128)(2,1)}), bf16[256,4096]{0,1:T(8,128)(2,1)}) %all-gather.17.cloned.1.call-update) | async-done | bytes 2097168 | tf_op jit(solution)/shard_map/all_gather | solution.py:86
  321.9 4.3 fusion.2
  326.2 0.0 reduce-scatter.2.cloned.1.call-update
  326.2 150.6 %reduce-scatter.2.cloned.1.call-done = f32[192,64]{0,1:T(8,128)} async-done(((f32[192,4096]{0,1:T(8,128)}), f32[192,64]{0,1:T(8,128)}) %reduce-scatter.2.cloned.1.call-update) | async-done | bytes 49168 | tf_op jit(solution)/shard_map/reduce_scatter | solution.py:89
  476.8 1.5 convert_element_type.27
  (8 shorter events, 0.1 us)
Async XLA Ops:
  6.5 32.5 %copy-start.1 = (bf16[256,512]{1,0:T(8,128)(2,1)S(1)}, bf16[256,512]{1,0:T(8,128)(2,1)}, u32[]{:S(2)}) copy-start(bf16[256,512]{1,0:T(8,128)(2,1)} %param.16) | copy-start | bytes 786436
  6.5 50.9 %copy-start.3 = (s32[128]{0:T(128)S(1)}, s32[128]{0:T(128)}, u32[]{:S(2)}) copy-start(s32[128]{0:T(128)} %param.17) | copy-start | bytes 1540
  6.5 120.6 %all-gather.7.cloned.1.call-start = ((), (), s32[]{:S(2)}) async-start(), calls=%async_computation.7 | async-start | bytes 2129920 | tf_op jit(solution)/shard_map/all_gather | solution.py:31
  7.3 136.1 %all-gather.9.cloned.1.call-start = ((), (), s32[]{:S(2)}) async-start(), calls=%async_computation.8 | async-start | bytes 2359296 | tf_op jit(solution)/shard_map/all_gather | solution.py:51
  8.0 180.2 %all-gather.13.cloned.1.call-start = ((), (), s32[]{:S(2)}) async-start(), calls=%async_computation.10 | async-start | bytes 2359296 | tf_op jit(solution)/shard_map/all_gather | solution.py:52
  10.5 22.2 %all-to-all-start = ((bf16[256,64,8]{0,2,1:T(8,128)(2,1)}), bf16[256,64,8]{0,2,1:T(8,128)(2,1)S(1)}, u32[]{:S(2)}, u32[]{:S(2)}) async-start(bf16[256,64,8]{0,2,1:T(8,128)(2,1)} %bitcast), calls=%async_computation | async-start | bytes 524288 | tf_op jit(solution)/shard_map/all_to_all | solution.py:34
  32.7 18.0 %all-to-all-start.2 = ((bf16[256,64,8]{0,2,1:T(8,128)(2,1)}), bf16[256,64,8]{0,2,1:T(8,128)(2,1)S(1)}, u32[]{:S(2)}, u32[]{:S(2)}) async-start(bf16[256,64,8]{0,2,1:T(8,128)(2,1)} %bitcast.7), calls=%async_computation.2 | async-start | bytes 524288 | tf_op jit(solution)/shard_map/all_to_all | solution.py:35
  50.7 18.4 %all-to-all-start.4 = ((bf16[256,64,8]{0,2,1:T(8,128)(2,1)}), bf16[256,64,8]{0,2,1:T(8,128)(2,1)S(1)}, u32[]{:S(2)}, u32[]{:S(2)}) async-start(bf16[256,64,8]{0,2,1:T(8,128)(2,1)} %bitcast.14), calls=%async_computation.4 | async-start | bytes 524288 | tf_op jit(solution)/shard_map/all_to_all | solution.py:36
  57.4 175.5 %all-gather.11.cloned.1.call-start = ((), (), s32[]{:S(2)}) async-start(), calls=%async_computation.9 | async-start | bytes 2359296 | tf_op jit(solution)/shard_map/all_gather | solution.py:53
  69.8 44.8 %copy-start.2 = (bf16[256,512]{1,0:T(8,128)(2,1)S(1)}, bf16[256,512]{1,0:T(8,128)(2,1)}, u32[]{:S(2)}) copy-start(bf16[256,512]{1,0:T(8,128)(2,1)} %param.15) | copy-start | bytes 786436
  89.8 187.8 %all-gather.15.cloned.1.call-start = ((), (), s32[]{:S(2)}) async-start(), calls=%async_computation.11 | async-start | bytes 2359296 | tf_op jit(solution)/shard_map/all_gather | solution.py:54
  108.2 18.0 %all-to-all-start.5 = ((bf16[64,256,8]{1,2,0:T(8,128)(2,1)}), bf16[64,256,8]{1,2,0:T(8,128)(2,1)S(1)}, u32[]{:S(2)}, u32[]{:S(2)}) async-start(bf16[64,256,8]{1,2,0:T(8,128)(2,1)} %bitcast.17), calls=%async_computation.5 | async-start | bytes 524288 | tf_op jit(solution)/shard_map/all_to_all | solution.py:45
  114.6 207.3 %all-gather.17.cloned.1.call-start = ((), (), s32[]{:S(2)}) async-start(), calls=%async_computation.12 | async-start | bytes 2359296 | tf_op jit(solution)/shard_map/all_gather | solution.py:86
  127.1 349.7 %reduce-scatter.2.cloned.1.call-start = ((), (), s32[]{:S(2)}) async-start(), calls=%async_computation.13 | async-start | bytes 4259840 | tf_op jit(solution)/shard_map/reduce_scatter | solution.py:89
  127.2 61.0 %copy-start = (bf16[192,4096]{0,1:T(8,128)(2,1)S(1)}, bf16[192,4096]{0,1:T(8,128)(2,1)}, u32[]{:S(2)}) copy-start(bf16[192,4096]{0,1:T(8,128)(2,1)} %all-gather.7.cloned.1.call-done) | copy-start | bytes 4718596
Sparse Core Ops, SparseCore 0:
  10.7 88.4 all-gather.6
  101.3 41.9 all-gather.8
  145.4 42.7 all-gather.12
  190.2 42.7 all-gather.10
  234.8 42.7 all-gather.14
  279.5 42.3 all-gather.16
  326.6 150.1 reduce-scatter.1
where the time goes:
time: 486 us; the launch traced here: 485 us
  waiting for transfers between devices  349 us (72%)
  blocking collectives  67.8 us (14%)
  starting transfers between devices  30 us (6%)
  matrix products  14.7 us (3%)
  between operations  13.6 us (3%)
  local copies, waits for them, and re-layouts  6.64 us (1%)
    reduce_scatter x1, waiting for transfers between devices, local(): lax.psum_scatter(partial_out, 'wid', scatter_dimension=1, tiled=True)  151 us
    all_gather x1, waiting for transfers between devices, local(): lax.all_gather(gate_src, 'tok', axis=1, tiled=True)  42.3 us
    all_gather x1, waiting for transfers between devices, local(): lax.all_gather(up_src, 'tok', axis=1, tiled=True)  42.2 us
    all_gather x1, waiting for transfers between devices, local(): lax.all_gather(up_a, 'tok', axis=1, tiled=True)  41.8 us
    all_to_all x1, blocking collectives, local(): lax.all_to_all(reorder_blocks(shipped[0], block_perm), 'wid', split_axis=...  19 us
    all_to_all x1, blocking collectives, local(): lax.all_to_all(reorder_blocks(shipped[1], block_perm), 'wid', split_axis=...  18.3 us
    all_gather x1, waiting for transfers between devices, local(): lax.all_gather(gate_a, 'tok', axis=1, tiled=True)  16.2 us
    psum x1, blocking collectives, local(): lax.psum((jnp.sum(hid_a, axis=0), jnp.sum(hid_b, axis=0), jnp.sum(hid_m,...  15.7 us
  transfers between devices with their start and end apart: 11, of which 10 were waited for; matrix products, arithmetic and copies ran while one was open for 4% of the time, Pallas kernels for 0%

commit v1 on v0

v1 whole, which is shorter than its diff:
```python
import functools

import jax
import jax.numpy as jnp
from jax import lax
from jax.experimental import pallas as pl
from jax.experimental.pallas import tpu as pltpu
from jax.sharding import PartitionSpec as P

NB = 128
GROUPS = 4
F32 = jnp.float32
BF16 = jnp.bfloat16
MESH_IDS = pl.DeviceIdType.MESH
VMEM_BYTES = 56 * 1024 * 1024


def copy_to(src, dst, send, recv, z, w):
    return pltpu.make_async_remote_copy(
        src_ref=src, dst_ref=dst, send_sem=send, recv_sem=recv, device_id=(z, w), device_id_type=MESH_IDS
    )


def signal(sem, z, w):
    pl.semaphore_signal(sem, inc=1, device_id=(z, w), device_id_type=MESH_IDS)


def position():
    z, w = lax.axis_index("tok"), lax.axis_index("wid")
    return z, w, w // 16, (w // 2) % 8, w % 2


def piece_of(x, y, c):
    return 4 * x + y // 2, 2 * c + y % 2


def piece_home(z, w, h):
    m = (w % 8) // 2
    return w // 8, 4 * (2 * z + h) + 2 * (m % 2) + m // 2


def greet(barrier, z, w, x, y, c, others):
    for k in range(1, 8):
        signal(barrier, z, 16 * x + 2 * ((y + k) % 8) + c)
    for k in range(1, 4):
        signal(barrier, z, 16 * ((x + k) % 4) + 2 * y + c)
    signal(barrier, z, 16 * x + 2 * y + (1 - c))
    own = 0
    for oz, ow in others:
        same = jnp.logical_and(oz == z, ow == w)
        own = own + same.astype(jnp.int32)

        @pl.when(jnp.logical_not(same))
        def _():
            signal(barrier, oz, ow)

    pl.semaphore_wait(barrier, 13 - own)


def either_start(src, dst, send, recv, z, w, oz, ow):
    same = jnp.logical_and(oz == z, ow == w)

    @pl.when(same)
    def _():
        pltpu.make_async_copy(src, dst, recv).start()

    @pl.when(jnp.logical_not(same))
    def _():
        copy_to(src, dst, send, recv, oz, ow).start()


def either_wait_send(src, dst, send, recv, z, w, oz, ow):
    same = jnp.logical_and(oz == z, ow == w)

    @pl.when(jnp.logical_not(same))
    def _():
        copy_to(src, dst, send, recv, oz, ow).wait_send()


def tokens_kernel(t_ref, x_ref, landed, piece, send, recv, local_sem):
    z, w, x, y, c = position()
    q, m = piece_of(x, y, c)
    e = w % 2
    barrier = pltpu.get_barrier_semaphore()
    sources = [(q // 2, 8 * z + 2 * m + s) for s in range(2)]
    homes = [piece_home(z, w, h) for h in range(2)]
    greet(barrier, z, w, x, y, c, sources)
    for h in range(2):
        either_start(t_ref.at[h], landed.at[e], send.at[h], recv.at[e], z, w, *homes[h])
    for s in range(2):
        copy_to(t_ref.at[0], landed.at[s], send.at[0], recv.at[s], z, w).wait_recv()
    piece[...] = landed[0] + landed[1]
    spot = x_ref.at[pl.ds(pl.multiple_of(96 * q, 32), 96), pl.ds(pl.multiple_of(128 * m, 128), 128)]
    keep = pltpu.make_async_copy(piece, spot, local_sem)
    keep.start()
    rounds = [
        copy_to(piece, spot, send.at[1 + k], recv.at[1 + k], z, 16 * x + 2 * ((y + k) % 8) + c)
        for k in (4, 3, 5, 2, 6, 1, 7)
    ]
    for r in rounds:
        r.start()
    keep.wait()
    for r in rounds:
        r.wait_recv()
    slab = x_ref.at[pl.ds(pl.multiple_of(384 * x, 128), 384), pl.ds(pl.multiple_of(256 * c, 128), 256)]
    slabs = [
        copy_to(slab, slab, send.at[8 + k], recv.at[8 + k], z, 16 * ((x + k) % 4) + 2 * y + c)
        for k in (2, 1, 3)
    ]
    for r in slabs:
        r.start()
    for r in slabs:
        r.wait_recv()
    half = x_ref.at[:, pl.ds(pl.multiple_of(256 * c, 128), 256)]
    last = copy_to(half, half, send.at[12], recv.at[12], z, 16 * x + 2 * y + (1 - c))
    last.start()
    last.wait()
    for r in rounds + slabs:
        r.wait_send()
    for h in range(2):
        either_wait_send(t_ref.at[h], landed.at[e], send.at[h], recv.at[e], z, w, *homes[h])


def gather_tokens(tokens):
    e = lax.axis_index("wid") % 2
    wide = jnp.pad(tokens, ((0, 0), (0, 64)))
    wide = jnp.where(e == 0, wide, jnp.roll(wide, 64, axis=1)).reshape(2, 96, 128)
    return pl.pallas_call(
        tokens_kernel,
        out_shape=jax.ShapeDtypeStruct((1536, 512), BF16),
        in_specs=[pl.BlockSpec(memory_space=pltpu.VMEM)],
        out_specs=pl.BlockSpec(memory_space=pltpu.VMEM),
        scratch_shapes=[
            pltpu.VMEM((2, 96, 128), BF16),
            pltpu.VMEM((96, 128), BF16),
            pltpu.SemaphoreType.DMA((13,)),
            pltpu.SemaphoreType.DMA((13,)),
            pltpu.SemaphoreType.DMA,
        ],
        compiler_params=pltpu.CompilerParams(
            collective_id=0, has_side_effects=True, vmem_limit_bytes=VMEM_BYTES
        ),
        name="gather_tokens",
    )(wide)


def silu(v):
    return v / (1.0 + jnp.exp(-v))


def hidden_kernel(x_ref, w_ref, out_ref, got, sent, acc, hid, send, recv, ag_send, ag_recv):
    z, w, _, _, _ = position()
    toward = ((z + 1) % 8, (z + 7) % 8)
    barrier = pltpu.get_barrier_semaphore()
    for n in toward:
        signal(barrier, n, w)
    pl.semaphore_wait(barrier, 2)

    def product(owner, g):
        return lax.dot_general(
            w_ref[owner],
            x_ref[pl.ds(pl.multiple_of(384 * g, 128), 384), :],
            (((1,), (1,)), ((), ())),
            preferred_element_type=F32,
        )

    def hop(d, s, g):
        return copy_to(
            sent.at[d, s, g], got.at[d, s, g], send.at[d, s, g], recv.at[d, s, g], toward[d], w
        )

    def pass_on(d, s, g, add):
        owner = (z + 4 - s) % 8 if d == 0 else (z + 4 + s) % 8
        value = product(owner, g)
        if add:
            hop(d, s - 1, g).wait_recv()
            value = value + got[d, s - 1, g].astype(F32)
        sent[d, s, g] = value.astype(BF16)
        hop(d, s, g).start()

    @pl.loop(0, 2)
    def _(g):
        pass_on(0, 0, g, False)
        pass_on(1, 0, g + 2, False)

    @pl.loop(0, 2)
    def _(g):
        pass_on(0, 1, g + 2, False)
        pass_on(1, 1, g, False)

    @pl.loop(0, 2)
    def _(g):
        pass_on(0, 1, g, True)
        pass_on(1, 1, g + 2, True)

    for s in (2, 3):

        @pl.loop(0, 4)
        def _(g):
            pass_on(0, s, (g + 2) % 4, True)
            pass_on(1, s, g, True)

    @pl.loop(0, 4)
    def _(g):
        acc[g] = product(z, g)

    @pl.loop(0, 4)
    def _(g):
        hop(0, 3, g).wait_recv()
        hop(1, 3, g).wait_recv()
        total = acc[g] + got[0, 3, g].astype(F32) + got[1, 3, g].astype(F32)
        gate_a, up_a, gate_b, up_b = (total[32 * i : 32 * i + 32] for i in range(4))
        hid[0, g] = silu(gate_a) * up_a
        hid[1, g] = silu(gate_b) * up_b
        hid[2, g] = silu(0.5 * (gate_a + gate_b)) * (0.5 * (up_a + up_b))

    def stats(i):
        center = sum(jnp.sum(hid[i, g], axis=1, keepdims=True) for g in range(GROUPS)) / 1536.0
        spread = (
            sum(jnp.sum((hid[i, g] - center) ** 2, axis=1, keepdims=True) for g in range(GROUPS)) / 1536.0
        )
        return center, jnp.sqrt(spread + 1e-05)

    center_a, dev_a = stats(0)
    center_b, dev_b = stats(1)
    center_m, dev_m = stats(2)
    target_std = 0.5 * (dev_a + dev_b)
    target_mean = 0.5 * (center_a + center_b)
    for g in range(GROUPS):
        repaired = (hid[2, g] - center_m) / dev_m * target_std + target_mean
        out_ref[z, :, 384 * g : 384 * g + 384] = repaired.astype(BF16)

    def lap(d, s, h):
        slot = (z + 8 - s) % 8 if d == 0 else (z + s) % 8
        spot = out_ref.at[slot, :, pl.ds(768 * h, 768)]
        return copy_to(spot, spot, ag_send.at[d, s, h], ag_recv.at[d, s, h], toward[d], w)

    def arrived(d, s, h):
        slot = (z + 7 - s) % 8 if d == 0 else (z + 1 + s) % 8
        spot = out_ref.at[slot, :, pl.ds(768 * h, 768)]
        copy_to(spot, spot, ag_send.at[d, s, h], ag_recv.at[d, s, h], toward[d], w).wait_recv()

    laps = []
    for s in range(4):
        for i in range(2):
            for d in range(2):
                h = i if d == 0 else 1 - i
                if s == 3 and i == 1:
                    continue
                if s > 0:
                    arrived(d, s - 1, h)
                one = lap(d, s, h)
                one.start()
                laps.append(one)
    for d in range(2):
        arrived(d, 3, d)
        arrived(d, 2, 1 - d)
    for one in laps:
        one.wait_send()

    @pl.loop(0, 2)
    def _(g):
        hop(0, 0, g).wait_send()
        hop(1, 0, g + 2).wait_send()

    for s in (1, 2, 3):

        @pl.loop(0, 4)
        def _(g):
            hop(0, s, g).wait_send()
            hop(1, s, g).wait_send()


def hidden(x, weights):
    return pl.pallas_call(
        hidden_kernel,
        out_shape=jax.ShapeDtypeStruct((8, 32, 1536), BF16),
        in_specs=[pl.BlockSpec(memory_space=pltpu.VMEM)] * 2,
        out_specs=pl.BlockSpec(memory_space=pltpu.VMEM),
        scratch_shapes=[
            pltpu.VMEM((2, 4, GROUPS, 128, 384), BF16),
            pltpu.VMEM((2, 4, GROUPS, 128, 384), BF16),
            pltpu.VMEM((GROUPS, 128, 384), F32),
            pltpu.VMEM((3, GROUPS, 32, 384), F32),
            pltpu.SemaphoreType.DMA((2, 4, GROUPS)),
            pltpu.SemaphoreType.DMA((2, 4, GROUPS)),
            pltpu.SemaphoreType.DMA((2, 4, 2)),
            pltpu.SemaphoreType.DMA((2, 4, 2)),
        ],
        compiler_params=pltpu.CompilerParams(
            collective_id=1, has_side_effects=True, vmem_limit_bytes=VMEM_BYTES
        ),
        name="hidden",
    )(x, weights)


def merge_kernel(
    own_ref, other_ref, out_ref, c_got, x_sent, x_got, y_own, y_sent, y_got, final, send, recv
):
    z, w, x, y, c = position()
    q, m = piece_of(x, y, c)
    h = q % 2
    barrier = pltpu.get_barrier_semaphore()
    homes = [piece_home(z, w, i) for i in range(2)]
    targets = [(q // 2, 8 * z + 2 * m + s) for s in range(2)]
    greet(barrier, z, w, x, y, c, homes)
    order = (2, 1, 3, 0)
    swaps = []
    for k in order:
        at = (x + k) % 4
        swap = copy_to(
            other_ref.at[at], c_got.at[at], send.at[k], recv.at[k], z, 16 * x + 2 * y + (1 - c)
        )
        swap.start()
        swaps.append(swap)
    moves = []
    for swap, k in zip(swaps[:3], order[:3]):
        at = (x + k) % 4
        swap.wait_recv()
        x_sent[k - 1] = (own_ref[at] + c_got[at].astype(F32)).astype(BF16)
        move = copy_to(
            x_sent.at[k - 1], x_got.at[k - 1], send.at[3 + k], recv.at[3 + k], z, 16 * at + 2 * y + c
        )
        move.start()
        moves.append(move)
    swaps[3].wait_recv()
    for move in moves:
        move.wait_recv()
    for r in range(4):
        for l in range(2):
            rows, lanes = slice(96 * r, 96 * r + 96), slice(128 * l, 128 * l + 128)
            part = own_ref[x, rows, lanes] + c_got[x, rows, lanes].astype(F32)
            for k in range(3):
                part = part + x_got[k, rows, lanes].astype(F32)
            y_own[2 * r + l] = part
            y_sent[2 * r + l] = part.astype(BF16)
    for k in (4, 3, 5, 2, 6, 1, 7):
        at = (y + k) % 8
        move = copy_to(
            y_sent.at[at], y_got.at[k - 1], send.at[6 + k], recv.at[6 + k], z, 16 * x + 2 * at + c
        )
        move.start()
        moves.append(move)
    for move in moves[3:]:
        move.wait_recv()
    part = y_own[y]
    for k in range(7):
        part = part + y_got[k].astype(F32)
    final[...] = part.astype(BF16)
    for s in range(2):
        either_start(final, out_ref.at[h], send.at[14 + s], recv.at[14 + h], z, w, *targets[s])
    for i in range(2):
        copy_to(final, out_ref.at[i], send.at[14], recv.at[14 + i], z, w).wait_recv()
    for s in range(2):
        either_wait_send(final, out_ref.at[h], send.at[14 + s], recv.at[14 + h], z, w, *targets[s])
    for move in swaps + moves:
        move.wait_send()


def merge(own, other):
    return pl.pallas_call(
        merge_kernel,
        out_shape=jax.ShapeDtypeStruct((2, 96, 128), BF16),
        in_specs=[pl.BlockSpec(memory_space=pltpu.VMEM)] * 2,
        out_specs=pl.BlockSpec(memory_space=pltpu.VMEM),
        scratch_shapes=[
            pltpu.VMEM((4, 384, 256), BF16),
            pltpu.VMEM((3, 384, 256), BF16),
            pltpu.VMEM((3, 384, 256), BF16),
            pltpu.VMEM((8, 96, 128), F32),
            pltpu.VMEM((8, 96, 128), BF16),
            pltpu.VMEM((7, 96, 128), BF16),
            pltpu.VMEM((96, 128), BF16),
            pltpu.SemaphoreType.DMA((16,)),
            pltpu.SemaphoreType.DMA((16,)),
        ],
        compiler_params=pltpu.CompilerParams(
            collective_id=2, has_side_effects=True, vmem_limit_bytes=VMEM_BYTES
        ),
        name="merge",
    )(own, other)


def spread_rows(matrices):
    stacked = jnp.stack(matrices).reshape(6, 2, 64, 2, 512).transpose(2, 0, 1, 3, 4)
    dealt = lax.all_to_all(stacked, "wid", split_axis=0, concat_axis=0, tiled=True)
    return dealt.transpose(1, 0, 2, 3, 4).reshape(6, NB, 2, 512)


def local(tokens, gate_a, up_a, gate_b, up_b, down_a, down_b, block_perm):
    c = lax.axis_index("wid") % 2
    x = gather_tokens(tokens)
    rows = spread_rows((gate_a, up_a, gate_b, up_b, down_a, down_b))
    take = functools.partial(jnp.take, indices=block_perm, axis=0)
    weights = jnp.stack((rows[0], rows[1], take(rows[2]), take(rows[3])))
    weights = weights.reshape(4, 8, 32, 512).transpose(1, 0, 2, 3).reshape(8, 128, 512)
    down_mid = ((rows[4].astype(F32) + take(rows[5]).astype(F32)) * 0.5).astype(BF16).reshape(256, 512)
    repaired = hidden(x, weights).reshape(256, 1536)

    def share(which):
        part = lax.dynamic_slice_in_dim(down_mid, 256 * which, 256, 1)
        return lax.dot_general(
            repaired, part, (((0,), (0,)), ((), ())), preferred_element_type=F32
        ).reshape(4, 384, 256)

    merged = merge(share(c), share(1 - c).astype(BF16)).reshape(192, 128)
    return jnp.where(c == 0, merged[:, :64], merged[:, 64:])


def solution(mesh):
    return jax.shard_map(
        local,
        mesh=mesh,
        in_specs=(
            P("tok", "wid"),
            P("wid", "tok"),
            P("wid", "tok"),
            P("wid", "tok"),
            P("wid", "tok"),
            P("wid", "tok"),
            P("wid", "tok"),
            P(),
        ),
        out_specs=P("tok", "wid"),
        check_vma=False,
    )
```

time: 486 us -> 186 us (0.38)
  the two profiles are of different devices: /device:TPU:16 before, /device:TPU:5 now
where the time goes in v1:
time: 186 us; the launch traced here: 185 us
  Pallas kernels  153 us (82%)
  local copies, waits for them, and re-layouts  15.2 us (8%)
  starting transfers between devices  11.2 us (6%)
  other arithmetic  2.84 us (2%)
  matrix products  2.76 us (1%)
    pallas_call x1, Pallas kernels, gather_tokens(): pl.pallas_call(tokens_kernel, out_shape=jax.ShapeDtypeStruct((1536, 512),...  66.2 us
    pallas_call x1, Pallas kernels, hidden(): pl.pallas_call(hidden_kernel, out_shape=jax.ShapeDtypeStruct((8, 32, 1536...  50.3 us
    pallas_call x1, Pallas kernels, merge(): pl.pallas_call(merge_kernel, out_shape=jax.ShapeDtypeStruct((2, 96, 128),...  36.3 us
    all_to_all x1, starting transfers between devices, spread_rows(): lax.all_to_all(stacked, 'wid', split_axis=0, concat_axis=0, tiled=True)  11.2 us
    another operation x7, local copies, waits for them, and re-layouts, spread_rows(): jnp.stack(matrices).reshape(6, 2, 64, 2, 512).transpose(2, 0, 1, 3, 4)  3.75 us
  transfers between devices with their start and end apart: 1, of which 0 were waited for; matrix products, arithmetic and copies ran while one was open for 0% of the time, Pallas kernels for 36%

profile of v1, /device:TPU:5, one launch (start us, length us, event | category | flops | bytes accessed | tf_op | source)
XLA Modules:
  0.0 185.2 jit_solution(592837263488867286)
XLA Ops:
  0.0 0.0 copy-start
  0.0 0.0 copy-start.1
  0.0 0.0 copy-start.2
  0.0 1.1 stack.34
  1.1 1.1 stack.35
  2.2 1.1 stack.36
  3.3 0.0 copy-done
  3.3 0.1 stack.37
  3.4 0.0 copy-done.1
  3.4 0.1 stack.38
  3.5 0.0 copy-done.2
  3.5 0.1 stack.39
  3.6 0.2 constant_dynamic-update-slice_fusion.5
  3.8 0.2 constant_dynamic-update-slice_fusion.4
  4.0 0.2 constant_dynamic-update-slice_fusion.3
  4.2 0.2 constant_dynamic-update-slice_fusion.2
  4.4 0.2 constant_dynamic-update-slice_fusion.1
  4.6 0.2 constant_dynamic-update-slice_fusion
  4.8 2.2 %copy.39 = bf16[64,6,2,2,512]{4,3,2,1,0:T(2,128)(2,1)} copy(bf16[64,6,2,2,512]{4,3,0,2,1:T(2,128)(2,1)S(1)} %bitcast.38) | data formatting | bytes 3145728 | tf_op jit(solution)/shard_map/transpose | solution.py:385
  7.1 0.0 copy-start.3
  7.1 11.2 %all-to-all-start = ((bf16[64,6,2,2,512]{4,3,2,1,0:T(2,128)(2,1)}), bf16[64,6,2,2,512]{4,3,2,1,0:T(2,128)(2,1)S(1)}, u32[]{:S(2)}, u32[]{:S(2)}) async-start(bf16[64,6,2,2,512]{4,3,2,1,0:T(2,128)(2,1)} %copy.39), calls=%async_computation | async-start | bytes 3145728 | tf_op jit(solution)/shard_map/all_to_all | solution.py:386
  18.2 0.0 copy-start.4
  18.3 0.0 copy-done.3
  18.3 0.7 copy.38
  19.0 66.2 %gather_tokens.1.x_ref = bf16[1536,512]{1,0:T(8,128)(2,1)} custom-call(bf16[2,96,128]{2,1,0:T(8,128)(2,1)} %bitcast.47), custom_call_target="tpu_custom_call" | custom-call | tf_op jit(solution)/shard_map/gather_tokens/pallas_call | solution.py:128
  85.3 0.0 copy-done.4
  85.3 0.0 all-to-all-done
  85.3 1.1 fusion.9
  86.4 1.1 gather_fusion.2
  87.6 0.5 fusion.1
  88.1 0.1 reshape.62
  88.2 1.1 gather_fusion.1
  89.3 1.1 gather_fusion
  90.5 0.6 broadcast_select_fusion.2
  91.0 0.1 stack.43
  91.1 0.1 stack.44
  91.3 0.1 stack.42
  91.4 0.1 stack.41
  91.5 1.1 pad_maximum_fusion
  92.6 50.3 %hidden.1 = bf16[8,32,1536]{2,1,0:T(8,128)(2,1)} custom-call(bf16[1536,512]{1,0:T(8,128)(2,1)} %gather_tokens.1.x_ref, bf16[8,128,512]{2,1,0:T(8,128)(2,1)} %bitcast.36), custom_call_target="tpu_custom_call" | custom-call | tf_op jit(solution)/shard_map/hidden/pallas_call | solution.py:275
  142.9 1.4 copy.44
  144.3 1.2 convolution_convert_fusion.other_ref
  145.5 1.5 fusion.3.own_ref
  147.0 36.3 %merge.1 = bf16[2,96,128]{2,1,0:T(8,128)(2,1)} custom-call(f32[4,384,256]{2,1,0:T(8,128)} %fusion.3.own_ref, bf16[4,384,256]{2,1,0:T(8,128)(2,1)} %convolution_convert_fusion.other_ref), custom_call_target="tpu_custom_call" | custom-call | tf_op jit(solution)/shard_map/merge/pallas_call | solution.py:361
  183.4 1.0 fusion.10
  184.3 0.1 copy.48
  184.4 0.1 copy.47
  184.5 0.6 broadcast_select_fusion.3
  (4 shorter events, 0.0 us)
Async XLA Ops:
  0.0 3.3 %copy-start = (bf16[256,512]{1,0:T(8,128)(2,1)S(1)}, bf16[256,512]{1,0:T(8,128)(2,1)}, u32[]{:S(2)}) copy-start(bf16[256,512]{1,0:T(8,128)(2,1)} %param.14) | copy-start | bytes 786436
  0.0 3.4 %copy-start.1 = (bf16[256,512]{1,0:T(8,128)(2,1)S(1)}, bf16[256,512]{1,0:T(8,128)(2,1)}, u32[]{:S(2)}) copy-start(bf16[256,512]{1,0:T(8,128)(2,1)} %param.15) | copy-start | bytes 786436
  0.0 3.5 %copy-start.2 = (bf16[256,512]{1,0:T(8,128)(2,1)S(1)}, bf16[256,512]{1,0:T(8,128)(2,1)}, u32[]{:S(2)}) copy-start(bf16[256,512]{1,0:T(8,128)(2,1)} %param.16) | copy-start | bytes 786436
  7.1 11.2 %copy-start.3 = (bf16[192,64]{0,1:T(8,128)(2,1)S(1)}, bf16[192,64]{0,1:T(8,128)(2,1)}, u32[]{:S(2)}) copy-start(bf16[192,64]{0,1:T(8,128)(2,1)} %param.10) | copy-start | bytes 73732
  7.1 78.3 %all-to-all-start = ((bf16[64,6,2,2,512]{4,3,2,1,0:T(2,128)(2,1)}), bf16[64,6,2,2,512]{4,3,2,1,0:T(2,128)(2,1)S(1)}, u32[]{:S(2)}, u32[]{:S(2)}) async-start(bf16[64,6,2,2,512]{4,3,2,1,0:T(2,128)(2,1)} %copy.39), calls=%async_computation | async-start | bytes 3145728 | tf_op jit(solution)/shard_map/all_to_all | solution.py:386
  18.2 67.1 %copy-start.4 = (s32[128]{0:T(128)S(1)}, s32[128]{0:T(128)}, u32[]{:S(2)}) copy-start(s32[128]{0:T(128)} %param.17) | copy-start | bytes 1540

commit v2 on v1

--- a/solution.py
+++ b/solution.py
@@ -102,17 +102,27 @@
     keep.wait()
     for r in rounds:
         r.wait_recv()
-    slab = x_ref.at[pl.ds(pl.multiple_of(384 * x, 128), 384), pl.ds(pl.multiple_of(256 * c, 128), 256)]
-    slabs = [
-        copy_to(slab, slab, send.at[8 + k], recv.at[8 + k], z, 16 * ((x + k) % 4) + 2 * y + c)
-        for k in (2, 1, 3)
-    ]
+    lanes = pl.ds(pl.multiple_of(256 * c, 128), 256)
+
+    def slab(xs, start, size):
+        return x_ref.at[pl.ds(pl.multiple_of(384 * xs + start, 64), size), lanes]
+
+    def x_move(spot, i, d):
+        to = (x + 1 + 2 * d) % 4
+        return copy_to(spot, spot, send.at[9 + i], recv.at[9 + i], z, 16 * to + 2 * y + c)
+
+    slabs = [x_move(slab(x, 192 * p, 192), 2 * d + p, d) for p, d in ((0, 0), (1, 1), (1, 0), (0, 1))]
     for r in slabs:
         r.start()
-    for r in slabs:
+    for d in range(2):
+        slabs[d].wait_recv()
+        on = x_move(slab((x + 3 + 2 * d) % 4, 192 * d, 192), 4 + d, d)
+        on.start()
+        slabs.append(on)
+    for r in slabs[2:]:
         r.wait_recv()
     half = x_ref.at[:, pl.ds(pl.multiple_of(256 * c, 128), 256)]
-    last = copy_to(half, half, send.at[12], recv.at[12], z, 16 * x + 2 * y + (1 - c))
+    last = copy_to(half, half, send.at[15], recv.at[15], z, 16 * x + 2 * y + (1 - c))
     last.start()
     last.wait()
     for r in rounds + slabs:
@@ -133,8 +143,8 @@
         scratch_shapes=[
             pltpu.VMEM((2, 96, 128), BF16),
             pltpu.VMEM((96, 128), BF16),
-            pltpu.SemaphoreType.DMA((13,)),
-            pltpu.SemaphoreType.DMA((13,)),
+            pltpu.SemaphoreType.DMA((16,)),
+            pltpu.SemaphoreType.DMA((16,)),
             pltpu.SemaphoreType.DMA,
         ],
         compiler_params=pltpu.CompilerParams(
@@ -148,14 +158,7 @@
     return v / (1.0 + jnp.exp(-v))
 
 
-def hidden_kernel(x_ref, w_ref, out_ref, got, sent, acc, hid, send, recv, ag_send, ag_recv):
-    z, w, _, _, _ = position()
-    toward = ((z + 1) % 8, (z + 7) % 8)
-    barrier = pltpu.get_barrier_semaphore()
-    for n in toward:
-        signal(barrier, n, w)
-    pl.semaphore_wait(barrier, 2)
-
+def ring_sum(x_ref, w_ref, got, sent, acc, send, recv, z, w, toward):
     def product(owner, g):
         return lax.dot_general(
             w_ref[owner],
@@ -208,8 +211,71 @@
     def _(g):
         hop(0, 3, g).wait_recv()
         hop(1, 3, g).wait_recv()
-        total = acc[g] + got[0, 3, g].astype(F32) + got[1, 3, g].astype(F32)
-        gate_a, up_a, gate_b, up_b = (total[32 * i : 32 * i + 32] for i in range(4))
+        acc[g] = acc[g] + got[0, 3, g].astype(F32) + got[1, 3, g].astype(F32)
+
+    def finish():
+        @pl.loop(0, 2)
+        def _(g):
+            hop(0, 0, g).wait_send()
+            hop(1, 0, g + 2).wait_send()
+
+        for s in (1, 2, 3):
+
+            @pl.loop(0, 4)
+            def _(g):
+                hop(0, s, g).wait_send()
+                hop(1, s, g).wait_send()
+
+    return finish
+
+
+def ring_entry():
+    z, w, _, _, _ = position()
+    toward = ((z + 1) % 8, (z + 7) % 8)
+    barrier = pltpu.get_barrier_semaphore()
+    for n in toward:
+        signal(barrier, n, w)
+    pl.semaphore_wait(barrier, 2)
+    return z, w, toward
+
+
+RING_SCRATCH = [
+    pltpu.VMEM((2, 4, GROUPS, 64, 384), BF16),
+    pltpu.VMEM((2, 4, GROUPS, 64, 384), BF16),
+    pltpu.SemaphoreType.DMA((2, 4, GROUPS)),
+    pltpu.SemaphoreType.DMA((2, 4, GROUPS)),
+]
+RING_COST = pl.CostEstimate(flops=20_000_000_000, bytes_accessed=60_000_000, transcendentals=0)
+
+
+def first_kernel(x_ref, w_ref, sum_ref, got, sent, send, recv):
+    z, w, toward = ring_entry()
+    ring_sum(x_ref, w_ref, got, sent, sum_ref, send, recv, z, w, toward)()
+
+
+def first_sums(x, weights):
+    return pl.pallas_call(
+        first_kernel,
+        out_shape=jax.ShapeDtypeStruct((GROUPS, 64, 384), F32),
+        in_specs=[pl.BlockSpec(memory_space=pltpu.VMEM)] * 2,
+        out_specs=pl.BlockSpec(memory_space=pltpu.VMEM),
+        scratch_shapes=RING_SCRATCH,
+        compiler_params=pltpu.CompilerParams(
+            collective_id=3, has_side_effects=True, vmem_limit_bytes=VMEM_BYTES
+        ),
+        cost_estimate=RING_COST,
+        name="first_sums",
+    )(x, weights)
+
+
+def hidden_kernel(x_ref, w_ref, a_ref, out_ref, got, sent, send, recv, acc, hid, ag_send, ag_recv):
+    z, w, toward = ring_entry()
+    finish = ring_sum(x_ref, w_ref, got, sent, acc, send, recv, z, w, toward)
+
+    @pl.loop(0, 4)
+    def _(g):
+        gate_a, up_a = a_ref[g, :32], a_ref[g, 32:]
+        gate_b, up_b = acc[g, :32], acc[g, 32:]
         hid[0, g] = silu(gate_a) * up_a
         hid[1, g] = silu(gate_b) * up_b
         hid[2, g] = silu(0.5 * (gate_a + gate_b)) * (0.5 * (up_a + up_b))
@@ -257,45 +323,32 @@
         arrived(d, 2, 1 - d)
     for one in laps:
         one.wait_send()
-
-    @pl.loop(0, 2)
-    def _(g):
-        hop(0, 0, g).wait_send()
-        hop(1, 0, g + 2).wait_send()
-
-    for s in (1, 2, 3):
-
-        @pl.loop(0, 4)
-        def _(g):
-            hop(0, s, g).wait_send()
-            hop(1, s, g).wait_send()
-
-
-def hidden(x, weights):
+    finish()
+
+
+def hidden(x, weights, sums_a):
     return pl.pallas_call(
         hidden_kernel,
         out_shape=jax.ShapeDtypeStruct((8, 32, 1536), BF16),
-        in_specs=[pl.BlockSpec(memory_space=pltpu.VMEM)] * 2,
+        in_specs=[pl.BlockSpec(memory_space=pltpu.VMEM)] * 3,
         out_specs=pl.BlockSpec(memory_space=pltpu.VMEM),
-        scratch_shapes=[
-            pltpu.VMEM((2, 4, GROUPS, 128, 384), BF16),
-            pltpu.VMEM((2, 4, GROUPS, 128, 384), BF16),
-            pltpu.VMEM((GROUPS, 128, 384), F32),
+        scratch_shapes=RING_SCRATCH
+        + [
+            pltpu.VMEM((GROUPS, 64, 384), F32),
             pltpu.VMEM((3, GROUPS, 32, 384), F32),
-            pltpu.SemaphoreType.DMA((2, 4, GROUPS)),
-            pltpu.SemaphoreType.DMA((2, 4, GROUPS)),
             pltpu.SemaphoreType.DMA((2, 4, 2)),
             pltpu.SemaphoreType.DMA((2, 4, 2)),
         ],
         compiler_params=pltpu.CompilerParams(
             collective_id=1, has_side_effects=True, vmem_limit_bytes=VMEM_BYTES
         ),
+        cost_estimate=RING_COST,
         name="hidden",
-    )(x, weights)
+    )(x, weights, sums_a)
 
 
 def merge_kernel(
-    own_ref, other_ref, out_ref, c_got, x_sent, x_got, y_own, y_sent, y_got, final, send, recv
+    own_ref, other_ref, out_ref, c_got, far_sent, far_got, near_sent, near_got, y_own, y_got, final, send, recv
 ):
     z, w, x, y, c = position()
     q, m = piece_of(x, y, c)
@@ -313,46 +366,63 @@
         )
         swap.start()
         swaps.append(swap)
+
+    def x_move(src, dst, i, d):
+        to = (x + 1 + 2 * d) % 4
+        return copy_to(src, dst, send.at[4 + i], recv.at[4 + i], z, 16 * to + 2 * y + c)
+
     moves = []
-    for swap, k in zip(swaps[:3], order[:3]):
-        at = (x + k) % 4
-        swap.wait_recv()
-        x_sent[k - 1] = (own_ref[at] + c_got[at].astype(F32)).astype(BF16)
-        move = copy_to(
-            x_sent.at[k - 1], x_got.at[k - 1], send.at[3 + k], recv.at[3 + k], z, 16 * at + 2 * y + c
-        )
+    swaps[0].wait_recv()
+    at = (x + 2) % 4
+    for d in range(2):
+        rows = slice(192 * d, 192 * d + 192)
+        far_sent[d] = (own_ref[at, rows] + c_got[at, rows]).astype(BF16)
+        move = x_move(far_sent.at[d], far_got.at[d], d, d)
         move.start()
         moves.append(move)
+    for d in range(2):
+        at = (x + 1 + 2 * d) % 4
+        swaps[1 + d].wait_recv()
+        for part in (1 - d, d):
+            rows = slice(192 * part, 192 * part + 192)
+            value = own_ref[at, rows] + c_got[at, rows]
+            if part == d:
+                moves[d].wait_recv()
+                value = value + far_got[d].astype(F32)
+            near_sent[d, part] = value.astype(BF16)
+            move = x_move(near_sent.at[d, part], near_got.at[d, part], 2 + 2 * d + part, d)
+            move.start()
+            moves.append(move)
     swaps[3].wait_recv()
-    for move in moves:
+    for move in moves[2:]:
         move.wait_recv()
     for r in range(4):
         for l in range(2):
             rows, lanes = slice(96 * r, 96 * r + 96), slice(128 * l, 128 * l + 128)
-            part = own_ref[x, rows, lanes] + c_got[x, rows, lanes].astype(F32)
-            for k in range(3):
-                part = part + x_got[k, rows, lanes].astype(F32)
+            inner = slice(96 * (r % 2), 96 * (r % 2) + 96)
+            part = own_ref[x, rows, lanes] + c_got[x, rows, lanes]
+            for d in range(2):
+                part = part + near_got[d, r // 2, inner, lanes].astype(F32)
             y_own[2 * r + l] = part
-            y_sent[2 * r + l] = part.astype(BF16)
     for k in (4, 3, 5, 2, 6, 1, 7):
         at = (y + k) % 8
         move = copy_to(
-            y_sent.at[at], y_got.at[k - 1], send.at[6 + k], recv.at[6 + k], z, 16 * x + 2 * at + c
+            y_own.at[at], y_got.at[k - 1], send.at[9 + k], recv.at[9 + k], z, 16 * x + 2 * at + c
         )
         move.start()
         moves.append(move)
-    for move in moves[3:]:
+    for move in moves[6:]:
         move.wait_recv()
     part = y_own[y]
     for k in range(7):
-        part = part + y_got[k].astype(F32)
+        part = part + y_got[k]
     final[...] = part.astype(BF16)
     for s in range(2):
-        either_start(final, out_ref.at[h], send.at[14 + s], recv.at[14 + h], z, w, *targets[s])
+        either_start(final, out_ref.at[h], send.at[17 + s], recv.at[17 + h], z, w, *targets[s])
     for i in range(2):
-        copy_to(final, out_ref.at[i], send.at[14], recv.at[14 + i], z, w).wait_recv()
+        copy_to(final, out_ref.at[i], send.at[17], recv.at[17 + i], z, w).wait_recv()
     for s in range(2):
-        either_wait_send(final, out_ref.at[h], send.at[14 + s], recv.at[14 + h], z, w, *targets[s])
+        either_wait_send(final, out_ref.at[h], send.at[17 + s], recv.at[17 + h], z, w, *targets[s])
     for move in swaps + moves:
         move.wait_send()
 
@@ -364,15 +434,16 @@
         in_specs=[pl.BlockSpec(memory_space=pltpu.VMEM)] * 2,
         out_specs=pl.BlockSpec(memory_space=pltpu.VMEM),
         scratch_shapes=[
-            pltpu.VMEM((4, 384, 256), BF16),
-            pltpu.VMEM((3, 384, 256), BF16),
-            pltpu.VMEM((3, 384, 256), BF16),
+            pltpu.VMEM((4, 384, 256), F32),
+            pltpu.VMEM((2, 192, 256), BF16),
+            pltpu.VMEM((2, 192, 256), BF16),
+            pltpu.VMEM((2, 2, 192, 256), BF16),
+            pltpu.VMEM((2, 2, 192, 256), BF16),
             pltpu.VMEM((8, 96, 128), F32),
-            pltpu.VMEM((8, 96, 128), BF16),
-            pltpu.VMEM((7, 96, 128), BF16),
+            pltpu.VMEM((7, 96, 128), F32),
             pltpu.VMEM((96, 128), BF16),
-            pltpu.SemaphoreType.DMA((16,)),
-            pltpu.SemaphoreType.DMA((16,)),
+            pltpu.SemaphoreType.DMA((19,)),
+            pltpu.SemaphoreType.DMA((19,)),
         ],
         compiler_params=pltpu.CompilerParams(
             collective_id=2, has_side_effects=True, vmem_limit_bytes=VMEM_BYTES
@@ -381,21 +452,29 @@
     )(own, other)
 
 
-def spread_rows(matrices):
-    stacked = jnp.stack(matrices).reshape(6, 2, 64, 2, 512).transpose(2, 0, 1, 3, 4)
+def spread_rows(*matrices):
+    stacked = jnp.stack(matrices).reshape(2, 2, 64, 2, 512).transpose(2, 0, 1, 3, 4)
     dealt = lax.all_to_all(stacked, "wid", split_axis=0, concat_axis=0, tiled=True)
-    return dealt.transpose(1, 0, 2, 3, 4).reshape(6, NB, 2, 512)
+    return dealt.transpose(1, 0, 2, 3, 4).reshape(2, NB, 2, 512)
+
+
+def by_owner(gate, up):
+    both = jnp.stack((gate, up)).reshape(2, 8, 32, 512)
+    return both.transpose(1, 0, 2, 3).reshape(8, 64, 512)
 
 
 def local(tokens, gate_a, up_a, gate_b, up_b, down_a, down_b, block_perm):
     c = lax.axis_index("wid") % 2
+    take = functools.partial(jnp.take, indices=block_perm, axis=0)
+    rows_a = spread_rows(gate_a, up_a)
     x = gather_tokens(tokens)
-    rows = spread_rows((gate_a, up_a, gate_b, up_b, down_a, down_b))
-    take = functools.partial(jnp.take, indices=block_perm, axis=0)
-    weights = jnp.stack((rows[0], rows[1], take(rows[2]), take(rows[3])))
-    weights = weights.reshape(4, 8, 32, 512).transpose(1, 0, 2, 3).reshape(8, 128, 512)
-    down_mid = ((rows[4].astype(F32) + take(rows[5]).astype(F32)) * 0.5).astype(BF16).reshape(256, 512)
-    repaired = hidden(x, weights).reshape(256, 1536)
+    gate_b, up_b, rows_a = lax.optimization_barrier((gate_b, up_b, rows_a))
+    rows_b = spread_rows(gate_b, up_b)
+    sums_a = first_sums(x, by_owner(rows_a[0], rows_a[1]))
+    down_a, down_b, rows_b = lax.optimization_barrier((down_a, down_b, rows_b))
+    rows_d = spread_rows(down_a, down_b)
+    repaired = hidden(x, by_owner(take(rows_b[0]), take(rows_b[1])), sums_a).reshape(256, 1536)
+    down_mid = ((rows_d[0].astype(F32) + take(rows_d[1]).astype(F32)) * 0.5).astype(BF16).reshape(256, 512)
 
     def share(which):
         part = lax.dynamic_slice_in_dim(down_mid, 256 * which, 256, 1)
@@ -403,7 +482,7 @@
             repaired, part, (((0,), (0,)), ((), ())), preferred_element_type=F32
         ).reshape(4, 384, 256)
 
-    merged = merge(share(c), share(1 - c).astype(BF16)).reshape(192, 128)
+    merged = merge(share(c), share(1 - c)).reshape(192, 128)
     return jnp.where(c == 0, merged[:, :64], merged[:, 64:])
 
 

time: 186 us -> 199 us (1.070)
  starting transfers between devices: 11.2 us -> 32 us
  Pallas kernels: 153 us -> 142 us
    pallas_call x1, Pallas kernels: 66.2 us -> 42 us  [gather_tokens(): pl.pallas_call(tokens_kernel, out_shape=jax.ShapeDtypeStruct((1536, 512),...]
    pallas_call x0 -> x1, Pallas kernels: none -> 22.3 us  [first_sums(): pl.pallas_call(first_kernel, out_shape=jax.ShapeDtypeStruct((GROUPS, 64,...]
    all_to_all x1 -> x3, starting transfers between devices: 11.2 us -> 32 us  [spread_rows(): lax.all_to_all(stacked, 'wid', split_axis=0, concat_axis=0, tiled=True)]
    pallas_call x1, Pallas kernels: 50.3 us -> 34.1 us  [hidden(): pl.pallas_call(hidden_kernel, out_shape=jax.ShapeDtypeStruct((8, 32, 1536...]
    pallas_call x1, Pallas kernels: 36.3 us -> 43.2 us  [merge(): pl.pallas_call(merge_kernel, out_shape=jax.ShapeDtypeStruct((2, 96, 128),...]
    transpose x1 -> x6, local copies, waits for them, and re-layouts: 2.23 us -> 5.13 us  [the longest x3 3.52 us: spread_rows(): jnp.stack(matrices).reshape(2, 2, 64, 2, 512).transpose(2, 0, 1, 3, 4)]
    transpose x0 -> x3, other arithmetic: none -> 2.22 us  [spread_rows(): jnp.stack(matrices).reshape(2, 2, 64, 2, 512).transpose(2, 0, 1, 3, 4)]
    another operation x11 -> x8, local copies, waits for them, and re-layouts: 4.16 us -> 2.73 us  [the longest x6 2.52 us: spread_rows(): jnp.stack(matrices).reshape(2, 2, 64, 2, 512).transpose(2, 0, 1, 3, 4)]
  transfers between devices with their start and end apart: 1 -> 3, of which waited for: 0 -> 0; matrix products, arithmetic and copies ran while one was open for 0% -> 2% of each run, Pallas kernels for 36% -> 50%
where the time goes in v2:
time: 199 us; the launch traced here: 198 us
  Pallas kernels  142 us (71%)
  starting transfers between devices  32 us (16%)
  local copies, waits for them, and re-layouts  16.2 us (8%)
  other arithmetic  4.8 us (2%)
  matrix products  3.05 us (2%)
    pallas_call x1, Pallas kernels, merge(): pl.pallas_call(merge_kernel, out_shape=jax.ShapeDtypeStruct((2, 96, 128),...  43.2 us
    pallas_call x1, Pallas kernels, gather_tokens(): pl.pallas_call(tokens_kernel, out_shape=jax.ShapeDtypeStruct((1536, 512),...  42 us
    pallas_call x1, Pallas kernels, hidden(): pl.pallas_call(hidden_kernel, out_shape=jax.ShapeDtypeStruct((8, 32, 1536...  34.1 us
    all_to_all x3, starting transfers between devices, spread_rows(): lax.all_to_all(stacked, 'wid', split_axis=0, concat_axis=0, tiled=True)  32 us
    pallas_call x1, Pallas kernels, first_sums(): pl.pallas_call(first_kernel, out_shape=jax.ShapeDtypeStruct((GROUPS, 64,...  22.3 us
  transfers between devices with their start and end apart: 3, of which 0 were waited for; matrix products, arithmetic and copies ran while one was open for 2% of the time, Pallas kernels for 50%

profile of v2, /device:TPU:5, one launch (start us, length us, event | category | flops | bytes accessed | tf_op | source)
XLA Modules:
  0.0 198.1 jit_solution(4346556783441347424)
XLA Ops:
  0.0 1.1 stack.37
  1.1 1.1 stack.38
  2.1 0.0 copy-start.4
  2.1 0.7 maximum_bitcast_fusion
  2.9 1.2 copy.39
  4.0 0.0 copy-start.5
  4.0 11.2 %all-to-all-start = ((bf16[64,2,2,2,512]{4,3,2,1,0:T(2,128)(2,1)}), bf16[64,2,2,2,512]{4,3,2,1,0:T(2,128)(2,1)S(1)}, u32[]{:S(2)}, u32[]{:S(2)}) async-start(bf16[64,2,2,2,512]{4,3,2,1,0:T(2,128)(2,1)} %copy.39), calls=%async_computation | async-start | bytes 1048576 | tf_op jit(solution)/shard_map/all_to_all | solution.py:457
  15.2 0.0 copy-start
  15.3 0.0 copy-done.4
  15.3 0.7 copy.38
  16.0 0.0 copy-start.1
  16.0 42.0 %gather_tokens.1.x_ref = bf16[1536,512]{1,0:T(8,128)(2,1)} custom-call(bf16[2,96,128]{2,1,0:T(8,128)(2,1)} %bitcast.57), custom_call_target="tpu_custom_call" | custom-call | tf_op jit(solution)/shard_map/gather_tokens/pallas_call | solution.py:138
  58.0 0.0 copy-done.5
  58.1 0.0 all-to-all-done
  58.1 0.4 copy.40
  58.5 0.0 copy-done
  58.5 0.1 stack.40
  58.6 0.0 copy-done.1
  58.6 0.1 stack.41
  58.7 0.7 maximum_bitcast_fusion.1
  59.4 1.2 copy.41
  60.6 8.6 %all-to-all-start.1 = ((bf16[64,2,2,2,512]{4,3,2,1,0:T(2,128)(2,1)}), bf16[64,2,2,2,512]{4,3,2,1,0:T(2,128)(2,1)S(1)}, u32[]{:S(2)}, u32[]{:S(2)}) async-start(bf16[64,2,2,2,512]{4,3,2,1,0:T(2,128)(2,1)} %copy.41), calls=%async_computation.1 | async-start | bytes 1048576 | tf_op jit(solution)/shard_map/all_to_all | solution.py:457
  69.2 0.8 copy.45
  70.1 0.9 copy.46
  71.0 22.3 %first_sums.1.a_ref = f32[4,64,384]{2,1,0:T(8,128)} custom-call(bf16[1536,512]{1,0:T(8,128)(2,1)} %gather_tokens.1.x_ref, bf16[8,64,512]{2,1,0:T(8,128)(2,1)} %bitcast.55), custom_call_target="tpu_custom_call" | custom-call | flops 20000000000 | bytes 60000000 | tf_op jit(solution)/shard_map/first_sums/pallas_call | solution.py:257
  93.2 0.0 all-to-all-done.1
  93.2 0.4 copy.42
  93.6 0.4 slice_bitcast_fusion.1
  94.0 0.0 copy-start.2
  94.0 1.1 gather_fusion
  95.1 0.0 copy-start.3
  95.1 1.1 gather_fusion.1
  96.3 0.6 broadcast_select_fusion.2
  96.8 0.1 stack.43
  97.0 0.1 stack.44
  97.1 0.0 copy-done.2
  97.1 0.1 stack.46
  97.2 0.0 copy-done.3
  97.2 0.1 stack.47
  97.3 0.7 maximum_bitcast_fusion.2
  98.1 1.2 copy.48
  99.2 12.2 %all-to-all-start.2 = ((bf16[64,2,2,2,512]{4,3,2,1,0:T(2,128)(2,1)}), bf16[64,2,2,2,512]{4,3,2,1,0:T(2,128)(2,1)S(1)}, u32[]{:S(2)}, u32[]{:S(2)}) async-start(bf16[64,2,2,2,512]{4,3,2,1,0:T(2,128)(2,1)} %copy.48), calls=%async_computation.2 | async-start | bytes 1048576 | tf_op jit(solution)/shard_map/all_to_all | solution.py:457
  111.5 0.8 pad_maximum_fusion
  112.3 34.1 %hidden.1 = bf16[8,32,1536]{2,1,0:T(8,128)(2,1)} custom-call(bf16[1536,512]{1,0:T(8,128)(2,1)} %gather_tokens.1.x_ref, bf16[8,64,512]{2,1,0:T(8,128)(2,1)} %bitcast.54, f32[4,64,384]{2,1,0:T(8,128)} %first_sums.1.a_ref), custom_call_target="tpu_custom_call" | custom-call | flops 20000000000 | bytes 60000000 | tf_op jit(solution)/shard_map/hidden/pallas_call | solution.py:330
  146.5 1.4 copy.47
  147.9 0.0 all-to-all-done.2
  147.9 0.4 fusion.10
  148.3 1.1 gather_fusion.2
  149.4 0.5 fusion.1
  149.9 0.1 reshape.70
  150.0 1.5 fusion.2.other_ref
  151.5 1.5 fusion.4.own_ref
  153.1 43.2 %merge.1 = bf16[2,96,128]{2,1,0:T(8,128)(2,1)} custom-call(f32[4,384,256]{2,1,0:T(8,128)} %fusion.4.own_ref, f32[4,384,256]{2,1,0:T(8,128)} %fusion.2.other_ref), custom_call_target="tpu_custom_call" | custom-call | tf_op jit(solution)/shard_map/merge/pallas_call | solution.py:431
  196.3 1.0 fusion.11
  197.2 0.1 copy.52
  197.3 0.1 copy.51
  197.4 0.6 broadcast_select_fusion.3
  (4 shorter events, 0.0 us)
Async XLA Ops:
  2.1 13.1 %copy-start.4 = (bf16[192,64]{0,1:T(8,128)(2,1)S(1)}, bf16[192,64]{0,1:T(8,128)(2,1)}, u32[]{:S(2)}) copy-start(bf16[192,64]{0,1:T(8,128)(2,1)} %param.10) | copy-start | bytes 73732
  4.0 54.0 %copy-start.5 = (s32[128]{0:T(128)S(1)}, s32[128]{0:T(128)}, u32[]{:S(2)}) copy-start(s32[128]{0:T(128)} %param.17) | copy-start | bytes 1540
  4.0 54.0 %all-to-all-start = ((bf16[64,2,2,2,512]{4,3,2,1,0:T(2,128)(2,1)}), bf16[64,2,2,2,512]{4,3,2,1,0:T(2,128)(2,1)S(1)}, u32[]{:S(2)}, u32[]{:S(2)}) async-start(bf16[64,2,2,2,512]{4,3,2,1,0:T(2,128)(2,1)} %copy.39), calls=%async_computation | async-start | bytes 1048576 | tf_op jit(solution)/shard_map/all_to_all | solution.py:457
  15.2 43.2 %copy-start = (bf16[256,512]{1,0:T(8,128)(2,1)S(1)}, bf16[256,512]{1,0:T(8,128)(2,1)}, u32[]{:S(2)}) copy-start(bf16[256,512]{1,0:T(8,128)(2,1)} %param.13) | copy-start | bytes 786436
  16.0 42.6 %copy-start.1 = (bf16[256,512]{1,0:T(8,128)(2,1)S(1)}, bf16[256,512]{1,0:T(8,128)(2,1)}, u32[]{:S(2)}) copy-start(bf16[256,512]{1,0:T(8,128)(2,1)} %param.14) | copy-start | bytes 786436
  60.6 32.6 %all-to-all-start.1 = ((bf16[64,2,2,2,512]{4,3,2,1,0:T(2,128)(2,1)}), bf16[64,2,2,2,512]{4,3,2,1,0:T(2,128)(2,1)S(1)}, u32[]{:S(2)}, u32[]{:S(2)}) async-start(bf16[64,2,2,2,512]{4,3,2,1,0:T(2,128)(2,1)} %copy.41), calls=%async_computation.1 | async-start | bytes 1048576 | tf_op jit(solution)/shard_map/all_to_all | solution.py:457
  94.0 3.1 %copy-start.2 = (bf16[256,512]{1,0:T(8,128)(2,1)S(1)}, bf16[256,512]{1,0:T(8,128)(2,1)}, u32[]{:S(2)}) copy-start(bf16[256,512]{1,0:T(8,128)(2,1)} %param.15) | copy-start | bytes 786436
  95.1 2.1 %copy-start.3 = (bf16[256,512]{1,0:T(8,128)(2,1)S(1)}, bf16[256,512]{1,0:T(8,128)(2,1)}, u32[]{:S(2)}) copy-start(bf16[256,512]{1,0:T(8,128)(2,1)} %param.16) | copy-start | bytes 786436
  99.2 48.7 %all-to-all-start.2 = ((bf16[64,2,2,2,512]{4,3,2,1,0:T(2,128)(2,1)}), bf16[64,2,2,2,512]{4,3,2,1,0:T(2,128)(2,1)S(1)}, u32[]{:S(2)}, u32[]{:S(2)}) async-start(bf16[64,2,2,2,512]{4,3,2,1,0:T(2,128)(2,1)} %copy.48), calls=%async_computation.2 | async-start | bytes 1048576 | tf_op jit(solution)/shard_map/all_to_all | solution.py:457

commit v3 on v2

--- a/solution.py
+++ b/solution.py
@@ -45,6 +45,10 @@
     for k in range(1, 4):
         signal(barrier, z, 16 * ((x + k) % 4) + 2 * y + c)
     signal(barrier, z, 16 * x + 2 * y + (1 - c))
+    greet_others(barrier, z, w, others, 11)
+
+
+def greet_others(barrier, z, w, others, already):
     own = 0
     for oz, ow in others:
         same = jnp.logical_and(oz == z, ow == w)
@@ -54,7 +58,7 @@
         def _():
             signal(barrier, oz, ow)
 
-    pl.semaphore_wait(barrier, 13 - own)
+    pl.semaphore_wait(barrier, already + len(others) - own)
 
 
 def either_start(src, dst, send, recv, z, w, oz, ow):
@@ -77,14 +81,37 @@
         copy_to(src, dst, send, recv, oz, ow).wait_send()
 
 
-def tokens_kernel(t_ref, x_ref, landed, piece, send, recv, local_sem):
+def deal(src, dst, send, recv, z, w, low, high, act):
+    @pl.loop(low, high)
+    def _(k):
+        to = (w + k) % 64
+        act(copy_to(src.at[to], dst.at[w], send.at[k], recv.at[k], z, to))
+
+
+def deal_start(src, dst, send, recv, z, w, low, high):
+    deal(src, dst, send, recv, z, w, low, high, lambda one: one.start())
+
+
+def deal_wait(src, dst, send, recv, z, w):
+    pltpu.make_async_copy(src.at[w], dst.at[w], recv.at[0]).wait()
+    deal(src, dst, send, recv, z, w, 1, 64, lambda one: one.wait())
+
+
+def greet_plane(barrier, z, w):
+    @pl.loop(1, 64)
+    def _(k):
+        signal(barrier, z, (w + k) % 64)
+
+
+def tokens_kernel(t_ref, r_ref, x_ref, dealt, landed, piece, send, recv, local_sem, d_send, d_recv):
     z, w, x, y, c = position()
     q, m = piece_of(x, y, c)
     e = w % 2
     barrier = pltpu.get_barrier_semaphore()
     sources = [(q // 2, 8 * z + 2 * m + s) for s in range(2)]
     homes = [piece_home(z, w, h) for h in range(2)]
-    greet(barrier, z, w, x, y, c, sources)
+    greet_plane(barrier, z, w)
+    greet_others(barrier, z, w, sources, 63)
     for h in range(2):
         either_start(t_ref.at[h], landed.at[e], send.at[h], recv.at[e], z, w, *homes[h])
     for s in range(2):
@@ -99,6 +126,8 @@
     ]
     for r in rounds:
         r.start()
+    pltpu.make_async_copy(r_ref.at[w], dealt.at[w], d_recv.at[0]).start()
+    deal_start(r_ref, dealt, d_send, d_recv, z, w, 1, 24)
     keep.wait()
     for r in rounds:
         r.wait_recv()
@@ -114,11 +143,13 @@
     slabs = [x_move(slab(x, 192 * p, 192), 2 * d + p, d) for p, d in ((0, 0), (1, 1), (1, 0), (0, 1))]
     for r in slabs:
         r.start()
+    deal_start(r_ref, dealt, d_send, d_recv, z, w, 24, 44)
     for d in range(2):
         slabs[d].wait_recv()
         on = x_move(slab((x + 3 + 2 * d) % 4, 192 * d, 192), 4 + d, d)
         on.start()
         slabs.append(on)
+    deal_start(r_ref, dealt, d_send, d_recv, z, w, 44, 64)
     for r in slabs[2:]:
         r.wait_recv()
     half = x_ref.at[:, pl.ds(pl.multiple_of(256 * c, 128), 256)]
@@ -127,31 +158,34 @@
     last.wait()
     for r in rounds + slabs:
         r.wait_send()
+    deal_wait(r_ref, dealt, d_send, d_recv, z, w)
     for h in range(2):
         either_wait_send(t_ref.at[h], landed.at[e], send.at[h], recv.at[e], z, w, *homes[h])
 
 
-def gather_tokens(tokens):
+def gather_tokens(tokens, rows):
     e = lax.axis_index("wid") % 2
     wide = jnp.pad(tokens, ((0, 0), (0, 64)))
     wide = jnp.where(e == 0, wide, jnp.roll(wide, 64, axis=1)).reshape(2, 96, 128)
     return pl.pallas_call(
         tokens_kernel,
-        out_shape=jax.ShapeDtypeStruct((1536, 512), BF16),
-        in_specs=[pl.BlockSpec(memory_space=pltpu.VMEM)],
-        out_specs=pl.BlockSpec(memory_space=pltpu.VMEM),
+        out_shape=(jax.ShapeDtypeStruct((1536, 512), BF16), jax.ShapeDtypeStruct(rows.shape, BF16)),
+        in_specs=[pl.BlockSpec(memory_space=pltpu.VMEM)] * 2,
+        out_specs=[pl.BlockSpec(memory_space=pltpu.VMEM)] * 2,
         scratch_shapes=[
             pltpu.VMEM((2, 96, 128), BF16),
             pltpu.VMEM((96, 128), BF16),
             pltpu.SemaphoreType.DMA((16,)),
             pltpu.SemaphoreType.DMA((16,)),
             pltpu.SemaphoreType.DMA,
+            pltpu.SemaphoreType.DMA((64,)),
+            pltpu.SemaphoreType.DMA((64,)),
         ],
         compiler_params=pltpu.CompilerParams(
             collective_id=0, has_side_effects=True, vmem_limit_bytes=VMEM_BYTES
         ),
         name="gather_tokens",
-    )(wide)
+    )(wide, rows)
 
 
 def silu(v):
@@ -229,53 +263,31 @@
     return finish
 
 
-def ring_entry():
+RING_SCRATCH = [
+    pltpu.VMEM((2, 4, GROUPS, 128, 384), BF16),
+    pltpu.VMEM((2, 4, GROUPS, 128, 384), BF16),
+    pltpu.SemaphoreType.DMA((2, 4, GROUPS)),
+    pltpu.SemaphoreType.DMA((2, 4, GROUPS)),
+]
+
+
+def hidden_kernel(
+    x_ref, w_ref, r_ref, out_ref, dealt, got, sent, send, recv, acc, hid, ag_send, ag_recv, d_send, d_recv
+):
     z, w, _, _, _ = position()
     toward = ((z + 1) % 8, (z + 7) % 8)
     barrier = pltpu.get_barrier_semaphore()
     for n in toward:
         signal(barrier, n, w)
-    pl.semaphore_wait(barrier, 2)
-    return z, w, toward
-
-
-RING_SCRATCH = [
-    pltpu.VMEM((2, 4, GROUPS, 64, 384), BF16),
-    pltpu.VMEM((2, 4, GROUPS, 64, 384), BF16),
-    pltpu.SemaphoreType.DMA((2, 4, GROUPS)),
-    pltpu.SemaphoreType.DMA((2, 4, GROUPS)),
-]
-RING_COST = pl.CostEstimate(flops=20_000_000_000, bytes_accessed=60_000_000, transcendentals=0)
-
-
-def first_kernel(x_ref, w_ref, sum_ref, got, sent, send, recv):
-    z, w, toward = ring_entry()
-    ring_sum(x_ref, w_ref, got, sent, sum_ref, send, recv, z, w, toward)()
-
-
-def first_sums(x, weights):
-    return pl.pallas_call(
-        first_kernel,
-        out_shape=jax.ShapeDtypeStruct((GROUPS, 64, 384), F32),
-        in_specs=[pl.BlockSpec(memory_space=pltpu.VMEM)] * 2,
-        out_specs=pl.BlockSpec(memory_space=pltpu.VMEM),
-        scratch_shapes=RING_SCRATCH,
-        compiler_params=pltpu.CompilerParams(
-            collective_id=3, has_side_effects=True, vmem_limit_bytes=VMEM_BYTES
-        ),
-        cost_estimate=RING_COST,
-        name="first_sums",
-    )(x, weights)
-
-
-def hidden_kernel(x_ref, w_ref, a_ref, out_ref, got, sent, send, recv, acc, hid, ag_send, ag_recv):
-    z, w, toward = ring_entry()
+    greet_plane(barrier, z, w)
+    pl.semaphore_wait(barrier, 65)
+    pltpu.make_async_copy(r_ref.at[w], dealt.at[w], d_recv.at[0]).start()
+    deal_start(r_ref, dealt, d_send, d_recv, z, w, 1, 64)
     finish = ring_sum(x_ref, w_ref, got, sent, acc, send, recv, z, w, toward)
 
     @pl.loop(0, 4)
     def _(g):
-        gate_a, up_a = a_ref[g, :32], a_ref[g, 32:]
-        gate_b, up_b = acc[g, :32], acc[g, 32:]
+        gate_a, up_a, gate_b, up_b = (acc[g, 32 * i : 32 * i + 32] for i in range(4))
         hid[0, g] = silu(gate_a) * up_a
         hid[1, g] = silu(gate_b) * up_b
         hid[2, g] = silu(0.5 * (gate_a + gate_b)) * (0.5 * (up_a + up_b))
@@ -324,27 +336,29 @@
     for one in laps:
         one.wait_send()
     finish()
-
-
-def hidden(x, weights, sums_a):
+    deal_wait(r_ref, dealt, d_send, d_recv, z, w)
+
+
+def hidden(x, weights, rows):
     return pl.pallas_call(
         hidden_kernel,
-        out_shape=jax.ShapeDtypeStruct((8, 32, 1536), BF16),
+        out_shape=(jax.ShapeDtypeStruct((8, 32, 1536), BF16), jax.ShapeDtypeStruct(rows.shape, BF16)),
         in_specs=[pl.BlockSpec(memory_space=pltpu.VMEM)] * 3,
-        out_specs=pl.BlockSpec(memory_space=pltpu.VMEM),
+        out_specs=[pl.BlockSpec(memory_space=pltpu.VMEM)] * 2,
         scratch_shapes=RING_SCRATCH
         + [
-            pltpu.VMEM((GROUPS, 64, 384), F32),
+            pltpu.VMEM((GROUPS, 128, 384), F32),
             pltpu.VMEM((3, GROUPS, 32, 384), F32),
             pltpu.SemaphoreType.DMA((2, 4, 2)),
             pltpu.SemaphoreType.DMA((2, 4, 2)),
+            pltpu.SemaphoreType.DMA((64,)),
+            pltpu.SemaphoreType.DMA((64,)),
         ],
         compiler_params=pltpu.CompilerParams(
             collective_id=1, has_side_effects=True, vmem_limit_bytes=VMEM_BYTES
         ),
-        cost_estimate=RING_COST,
         name="hidden",
-    )(x, weights, sums_a)
+    )(x, weights, rows)
 
 
 def merge_kernel(
@@ -452,29 +466,27 @@
     )(own, other)
 
 
-def spread_rows(*matrices):
-    stacked = jnp.stack(matrices).reshape(2, 2, 64, 2, 512).transpose(2, 0, 1, 3, 4)
-    dealt = lax.all_to_all(stacked, "wid", split_axis=0, concat_axis=0, tiled=True)
-    return dealt.transpose(1, 0, 2, 3, 4).reshape(2, NB, 2, 512)
-
-
-def by_owner(gate, up):
-    both = jnp.stack((gate, up)).reshape(2, 8, 32, 512)
-    return both.transpose(1, 0, 2, 3).reshape(8, 64, 512)
+def by_dest(*matrices):
+    n = len(matrices)
+    return jnp.stack(matrices).reshape(n, 2, 64, 2, 512).transpose(2, 0, 1, 3, 4)
+
+
+def by_block(dealt):
+    n = dealt.shape[1]
+    return dealt.transpose(1, 0, 2, 3, 4).reshape(n, NB, 2, 512)
 
 
 def local(tokens, gate_a, up_a, gate_b, up_b, down_a, down_b, block_perm):
     c = lax.axis_index("wid") % 2
     take = functools.partial(jnp.take, indices=block_perm, axis=0)
-    rows_a = spread_rows(gate_a, up_a)
-    x = gather_tokens(tokens)
-    gate_b, up_b, rows_a = lax.optimization_barrier((gate_b, up_b, rows_a))
-    rows_b = spread_rows(gate_b, up_b)
-    sums_a = first_sums(x, by_owner(rows_a[0], rows_a[1]))
-    down_a, down_b, rows_b = lax.optimization_barrier((down_a, down_b, rows_b))
-    rows_d = spread_rows(down_a, down_b)
-    repaired = hidden(x, by_owner(take(rows_b[0]), take(rows_b[1])), sums_a).reshape(256, 1536)
-    down_mid = ((rows_d[0].astype(F32) + take(rows_d[1]).astype(F32)) * 0.5).astype(BF16).reshape(256, 512)
+    x, rows = gather_tokens(tokens, by_dest(gate_a, up_a, gate_b, up_b))
+    rows = by_block(rows)
+    weights = jnp.stack((rows[0], rows[1], take(rows[2]), take(rows[3])))
+    weights = weights.reshape(4, 8, 32, 512).transpose(1, 0, 2, 3).reshape(8, 128, 512)
+    repaired, rows = hidden(x, weights, by_dest(down_a, down_b))
+    repaired = repaired.reshape(256, 1536)
+    rows = by_block(rows)
+    down_mid = ((rows[0].astype(F32) + take(rows[1]).astype(F32)) * 0.5).astype(BF16).reshape(256, 512)
 
     def share(which):
         part = lax.dynamic_slice_in_dim(down_mid, 256 * which, 256, 1)

time: 199 us -> 176 us (0.88)
  starting transfers between devices: 32 us -> 0 us
  Pallas kernels: 142 us -> 153 us
  local copies, waits for them, and re-layouts: 16.2 us -> 12.9 us
  other arithmetic: 4.8 us -> 7.14 us
    all_to_all x3 -> x0, starting transfers between devices: 32 us -> none  [spread_rows(): lax.all_to_all(stacked, 'wid', split_axis=0, concat_axis=0, tiled=True)]
    pallas_call x3 -> x2, Pallas kernels: 98.4 us -> 111 us  [the longest x1 56.2 us: hidden(): pl.pallas_call(hidden_kernel, out_shape=(jax.ShapeDtypeStruct((8, 32, 153...]
    transpose x6 -> x0, local copies, waits for them, and re-layouts: 5.13 us -> none  [the longest x3 3.52 us: spread_rows(): jnp.stack(matrices).reshape(2, 2, 64, 2, 512).transpose(2, 0, 1, 3, 4)]
    slice x1 -> x2, local copies, waits for them, and re-layouts: 0.36 us -> 3.4 us  [the longest x1 1.94 us: local(): weights = jnp.stack((rows[0], rows[1], take(rows[2]), take(rows[3])))]
  transfers between devices with their start and end apart: 3 -> 0, of which waited for: 0 -> 0; matrix products, arithmetic and copies ran while one was open for 2% -> 0% of each run, Pallas kernels for 50% -> 0%
where the time goes in v3:
time: 176 us
  Pallas kernels  153 us (87%)
  local copies, waits for them, and re-layouts  12.9 us (7%)
  other arithmetic  7.14 us (4%)
  matrix products  3.04 us (2%)
    pallas_call x1, Pallas kernels, hidden(): pl.pallas_call(hidden_kernel, out_shape=(jax.ShapeDtypeStruct((8, 32, 153...  56.2 us
    pallas_call x1, Pallas kernels, gather_tokens(): pl.pallas_call(tokens_kernel, out_shape=(jax.ShapeDtypeStruct((1536, 512)...  55.2 us
    pallas_call x1, Pallas kernels, merge(): pl.pallas_call(merge_kernel, out_shape=jax.ShapeDtypeStruct((2, 96, 128),...  41.2 us

profile of v3, /device:TPU:5, one launch (start us, length us, event | category | flops | bytes accessed | tf_op | source)
XLA Modules:
  0.0 175.9 jit_solution(17522403873877793746)
XLA Ops:
  0.0 0.0 copy-start.1
  0.0 0.8 pad_select_fusion
  0.9 0.7 copy.15
  1.6 1.1 stack.37
  2.6 1.1 stack.38
  3.7 1.1 stack.39
  4.7 0.0 copy-done.1
  4.7 0.1 stack.40
  4.9 2.2 %copy_bitcast_fusion.r_ref = bf16[64,4,2,2,512]{4,3,2,1,0:T(2,128)(2,1)} fusion(bf16[1,2,64,2,512]{4,3,2,1,0:T(2,128)(2,1)S(1)} %stack.40, bf16[1,2,64,2,512]{4,3,2,1,0:T(2,128)(2,1)S(1)} %stack.39, bf16[1,2,64,2,512]{4,3,2,1,0:T(2,128)(2,1)S(1)} %stack.38, bf16[1,2,64,2,512]{4,3,2,1,0:T(2,128)(2,1)S(1)} %stack.37), kind=kLoop, calls=%fused_computation.5 | loop fusion | flops 1572864 | bytes 2097152 | tf_op jit(solution)/shard_map/transpose | solution.py:471
  7.0 0.0 copy-start.4
  7.0 55.2 %gather_tokens.1 = (bf16[1536,512]{1,0:T(8,128)(2,1)}, bf16[64,4,2,2,512]{4,3,2,1,0:T(2,128)(2,1)}) custom-call(bf16[2,96,128]{2,1,0:T(8,128)(2,1)} %bitcast.47, bf16[64,4,2,2,512]{4,3,2,1,0:T(2,128)(2,1)} %copy_bitcast_fusion.r_ref), custom_call_target="tpu_custom_call" | custom-call | tf_op jit(solution)/shard_map/gather_tokens/pallas_call | solution.py:170
  62.2 1.9 %fusion.10 = (bf16[1,64,2,2,512]{4,3,2,0,1:T(2,128)(2,1)S(1)}, bf16[1,64,2,2,512]{4,3,2,0,1:T(2,128)(2,1)S(1)}, bf16[1,64,2,2,512]{4,3,2,0,1:T(2,128)(2,1)S(1)}, bf16[1,64,2,2,512]{4,3,2,0,1:T(2,128)(2,1)S(1)}) fusion(bf16[4,64,2,2,512]{4,3,2,0,1:T(2,128)(2,1)} %bitcast.38), kind=kLoop, calls=%fused_computation.27 | loop fusion | bytes 2097152 | tf_op jit(solution)/shard_map/slice | solution.py:484
  64.2 0.0 copy-done.4
  64.2 1.1 gather_fusion
  65.3 1.1 gather_fusion.1
  66.5 0.6 broadcast_select_fusion.2
  67.0 0.1 stack.44
  67.2 0.1 stack.45
  67.3 0.0 copy-start.2
  67.3 0.1 stack.42
  67.4 0.0 copy-start.3
  67.4 0.1 stack.43
  67.5 1.1 pad_maximum_fusion.1
  68.6 0.0 copy-done.2
  68.6 0.1 stack.47
  68.7 0.0 copy-done.3
  68.7 0.1 stack.48
  68.8 1.3 copy_bitcast_fusion.1.r_ref
  70.1 56.2 %hidden.1 = (bf16[8,32,1536]{2,1,0:T(8,128)(2,1)}, bf16[64,2,2,2,512]{4,3,2,1,0:T(2,128)(2,1)}) custom-call(bf16[1536,512]{1,0:T(8,128)(2,1)} %get-tuple-element.10.x_ref, bf16[8,128,512]{2,1,0:T(8,128)(2,1)} %bitcast.37, bf16[64,2,2,2,512]{4,3,2,1,0:T(2,128)(2,1)} %copy_bitcast_fusion.1.r_ref), custom_call_target="tpu_custom_call" | custom-call | tf_op jit(solution)/shard_map/hidden/pallas_call | solution.py:343
  126.3 0.0 copy-start
  126.3 1.5 fusion.11
  127.8 1.1 gather_fusion.2
  128.9 0.5 fusion.1
  129.5 0.1 reshape.64
  129.6 0.0 copy-done
  129.6 0.3 copy.24
  129.9 1.5 fusion.2.other_ref
  131.4 1.5 fusion.4.own_ref
  132.9 41.2 %merge.1 = bf16[2,96,128]{2,1,0:T(8,128)(2,1)} custom-call(f32[4,384,256]{2,1,0:T(8,128)} %fusion.4.own_ref, f32[4,384,256]{2,1,0:T(8,128)} %fusion.2.other_ref), custom_call_target="tpu_custom_call" | custom-call | tf_op jit(solution)/shard_map/merge/pallas_call | solution.py:445
  174.1 1.0 fusion.12
  175.1 0.1 copy.29
  175.2 0.1 copy.30
  175.3 0.6 broadcast_select_fusion.3
  (3 shorter events, 0.0 us)
Async XLA Ops:
  0.0 4.7 %copy-start.1 = (bf16[256,512]{1,0:T(8,128)(2,1)S(1)}, bf16[256,512]{1,0:T(8,128)(2,1)}, u32[]{:S(2)}) copy-start(bf16[256,512]{1,0:T(8,128)(2,1)} %param.14) | copy-start | bytes 786436
  7.0 57.1 %copy-start.4 = (s32[128]{0:T(128)S(1)}, s32[128]{0:T(128)}, u32[]{:S(2)}) copy-start(s32[128]{0:T(128)} %param.17) | copy-start | bytes 1540
  67.3 1.4 copy-start.2
  67.4 1.3 copy-start.3
  126.3 3.3 %copy-start = (bf16[8,32,1536]{2,1,0:T(8,128)(2,1)S(1)}, bf16[8,32,1536]{2,1,0:T(8,128)(2,1)}, u32[]{:S(2)}) copy-start(bf16[8,32,1536]{2,1,0:T(8,128)(2,1)} %get-tuple-element.12) | copy-start | bytes 2359300

commit v4 on v3

--- a/solution.py
+++ b/solution.py
@@ -114,6 +114,8 @@
     greet_others(barrier, z, w, sources, 63)
     for h in range(2):
         either_start(t_ref.at[h], landed.at[e], send.at[h], recv.at[e], z, w, *homes[h])
+    pltpu.make_async_copy(r_ref.at[w], dealt.at[w], d_recv.at[0]).start()
+    deal_start(r_ref, dealt, d_send, d_recv, z, w, 1, 12)
     for s in range(2):
         copy_to(t_ref.at[0], landed.at[s], send.at[0], recv.at[s], z, w).wait_recv()
     piece[...] = landed[0] + landed[1]
@@ -126,8 +128,7 @@
     ]
     for r in rounds:
         r.start()
-    pltpu.make_async_copy(r_ref.at[w], dealt.at[w], d_recv.at[0]).start()
-    deal_start(r_ref, dealt, d_send, d_recv, z, w, 1, 24)
+    deal_start(r_ref, dealt, d_send, d_recv, z, w, 12, 28)
     keep.wait()
     for r in rounds:
         r.wait_recv()
@@ -143,13 +144,13 @@
     slabs = [x_move(slab(x, 192 * p, 192), 2 * d + p, d) for p, d in ((0, 0), (1, 1), (1, 0), (0, 1))]
     for r in slabs:
         r.start()
-    deal_start(r_ref, dealt, d_send, d_recv, z, w, 24, 44)
+    deal_start(r_ref, dealt, d_send, d_recv, z, w, 28, 46)
     for d in range(2):
         slabs[d].wait_recv()
         on = x_move(slab((x + 3 + 2 * d) % 4, 192 * d, 192), 4 + d, d)
         on.start()
         slabs.append(on)
-    deal_start(r_ref, dealt, d_send, d_recv, z, w, 44, 64)
+    deal_start(r_ref, dealt, d_send, d_recv, z, w, 46, 64)
     for r in slabs[2:]:
         r.wait_recv()
     half = x_ref.at[:, pl.ds(pl.multiple_of(256 * c, 128), 256)]
@@ -192,7 +193,7 @@
     return v / (1.0 + jnp.exp(-v))
 
 
-def ring_sum(x_ref, w_ref, got, sent, acc, send, recv, z, w, toward):
+def ring_sum(x_ref, w_ref, got, sent, acc, send, recv, z, w, toward, beside):
     def product(owner, g):
         return lax.dot_general(
             w_ref[owner],
@@ -220,6 +221,8 @@
         pass_on(0, 0, g, False)
         pass_on(1, 0, g + 2, False)
 
+    beside(0)
+
     @pl.loop(0, 2)
     def _(g):
         pass_on(0, 1, g + 2, False)
@@ -230,12 +233,16 @@
         pass_on(0, 1, g, True)
         pass_on(1, 1, g + 2, True)
 
+    beside(1)
+
     for s in (2, 3):
 
         @pl.loop(0, 4)
         def _(g):
             pass_on(0, s, (g + 2) % 4, True)
             pass_on(1, s, g, True)
+
+        beside(s)
 
     @pl.loop(0, 4)
     def _(g):
@@ -282,8 +289,12 @@
     greet_plane(barrier, z, w)
     pl.semaphore_wait(barrier, 65)
     pltpu.make_async_copy(r_ref.at[w], dealt.at[w], d_recv.at[0]).start()
-    deal_start(r_ref, dealt, d_send, d_recv, z, w, 1, 64)
-    finish = ring_sum(x_ref, w_ref, got, sent, acc, send, recv, z, w, toward)
+
+    def beside(step):
+        bounds = (1, 17, 33, 49, 64)
+        deal_start(r_ref, dealt, d_send, d_recv, z, w, bounds[step], bounds[step + 1])
+
+    finish = ring_sum(x_ref, w_ref, got, sent, acc, send, recv, z, w, toward, beside)
 
     @pl.loop(0, 4)
     def _(g):
@@ -362,7 +373,7 @@
 
 
 def merge_kernel(
-    own_ref, other_ref, out_ref, c_got, far_sent, far_got, near_sent, near_got, y_own, y_got, final, send, recv
+    h_ref, own_w, other_w, out_ref, own_ref, other_ref, c_got, far_sent, far_got, near_sent, near_got, y_own, y_got, final, send, recv
 ):
     z, w, x, y, c = position()
     q, m = piece_of(x, y, c)
@@ -375,11 +386,16 @@
     swaps = []
     for k in order:
         at = (x + k) % 4
+        other_ref[at] = jnp.dot(h_ref[at], other_w[...], preferred_element_type=F32)
         swap = copy_to(
             other_ref.at[at], c_got.at[at], send.at[k], recv.at[k], z, 16 * x + 2 * y + (1 - c)
         )
         swap.start()
         swaps.append(swap)
+
+    for k in order:
+        at = (x + k) % 4
+        own_ref[at] = jnp.dot(h_ref[at], own_w[...], preferred_element_type=F32)
 
     def x_move(src, dst, i, d):
         to = (x + 1 + 2 * d) % 4
@@ -441,13 +457,15 @@
         move.wait_send()
 
 
-def merge(own, other):
+def merge(repaired, own, other):
     return pl.pallas_call(
         merge_kernel,
         out_shape=jax.ShapeDtypeStruct((2, 96, 128), BF16),
-        in_specs=[pl.BlockSpec(memory_space=pltpu.VMEM)] * 2,
+        in_specs=[pl.BlockSpec(memory_space=pltpu.VMEM)] * 3,
         out_specs=pl.BlockSpec(memory_space=pltpu.VMEM),
         scratch_shapes=[
+            pltpu.VMEM((4, 384, 256), F32),
+            pltpu.VMEM((4, 384, 256), F32),
             pltpu.VMEM((4, 384, 256), F32),
             pltpu.VMEM((2, 192, 256), BF16),
             pltpu.VMEM((2, 192, 256), BF16),
@@ -463,7 +481,7 @@
             collective_id=2, has_side_effects=True, vmem_limit_bytes=VMEM_BYTES
         ),
         name="merge",
-    )(own, other)
+    )(repaired, own, other)
 
 
 def by_dest(*matrices):
@@ -478,23 +496,20 @@
 
 def local(tokens, gate_a, up_a, gate_b, up_b, down_a, down_b, block_perm):
     c = lax.axis_index("wid") % 2
-    take = functools.partial(jnp.take, indices=block_perm, axis=0)
+    take = functools.partial(jnp.take, indices=block_perm, mode="clip")
     x, rows = gather_tokens(tokens, by_dest(gate_a, up_a, gate_b, up_b))
     rows = by_block(rows)
-    weights = jnp.stack((rows[0], rows[1], take(rows[2]), take(rows[3])))
+    weights = jnp.stack((rows[0], rows[1], take(rows[2], axis=0), take(rows[3], axis=0)))
     weights = weights.reshape(4, 8, 32, 512).transpose(1, 0, 2, 3).reshape(8, 128, 512)
     repaired, rows = hidden(x, weights, by_dest(down_a, down_b))
     repaired = repaired.reshape(256, 1536)
     rows = by_block(rows)
-    down_mid = ((rows[0].astype(F32) + take(rows[1]).astype(F32)) * 0.5).astype(BF16).reshape(256, 512)
-
-    def share(which):
-        part = lax.dynamic_slice_in_dim(down_mid, 256 * which, 256, 1)
-        return lax.dot_general(
-            repaired, part, (((0,), (0,)), ((), ())), preferred_element_type=F32
-        ).reshape(4, 384, 256)
-
-    merged = merge(share(c), share(1 - c)).reshape(192, 128)
+    down_mid = ((rows[0].astype(F32) + take(rows[1], axis=0).astype(F32)) * 0.5).astype(BF16).reshape(256, 512)
+
+    halves = (down_mid[:, :256], down_mid[:, 256:])
+    own = jnp.where(c == 0, *halves)
+    other = jnp.where(c == 0, *halves[::-1])
+    merged = merge(repaired.T.reshape(4, 384, 256), own, other).reshape(192, 128)
     return jnp.where(c == 0, merged[:, :64], merged[:, 64:])
 
 

time: 176 us -> 174 us (0.989)
  the two profiles are of different devices: /device:TPU:5 before, /device:TPU:11 now
where the time goes in v4:
time: 174 us; the launch traced here: 173 us
  Pallas kernels  151 us (87%)
  local copies, waits for them, and re-layouts  13.9 us (8%)
  other arithmetic  7.91 us (5%)
    pallas_call x1, Pallas kernels, gather_tokens(): pl.pallas_call(tokens_kernel, out_shape=(jax.ShapeDtypeStruct((1536, 512)...  55.6 us
    pallas_call x1, Pallas kernels, hidden(): pl.pallas_call(hidden_kernel, out_shape=(jax.ShapeDtypeStruct((8, 32, 153...  54.8 us
    pallas_call x1, Pallas kernels, merge(): pl.pallas_call(merge_kernel, out_shape=jax.ShapeDtypeStruct((2, 96, 128),...  40.6 us
    another operation x6, local copies, waits for them, and re-layouts, by_dest(): jnp.stack(matrices).reshape(n, 2, 64, 2, 512).transpose(2, 0, 1, 3, 4)  3.51 us

profile of v4, /device:TPU:11, one launch (start us, length us, event | category | flops | bytes accessed | tf_op | source)
XLA Modules:
  0.0 173.1 jit_solution(6390467880946464008)
XLA Ops:
  0.0 0.0 copy-start.1
  0.0 0.7 pad_clamp_fusion
  0.7 0.8 pad_select_fusion
  1.6 0.7 copy.15
  2.3 1.1 stack.37
  3.3 1.1 stack.38
  4.4 0.0 copy-start.2
  4.4 1.1 stack.39
  5.5 0.0 copy-done.1
  5.5 0.0 copy-start.3
  5.5 0.1 stack.40
  5.6 2.2 %copy_bitcast_fusion.r_ref = bf16[64,4,2,2,512]{4,3,2,1,0:T(2,128)(2,1)} fusion(bf16[1,2,64,2,512]{4,3,2,1,0:T(2,128)(2,1)S(1)} %stack.40, bf16[1,2,64,2,512]{4,3,2,1,0:T(2,128)(2,1)S(1)} %stack.39, bf16[1,2,64,2,512]{4,3,2,1,0:T(2,128)(2,1)S(1)} %stack.38, bf16[1,2,64,2,512]{4,3,2,1,0:T(2,128)(2,1)S(1)} %stack.37), kind=kLoop, calls=%fused_computation.5 | loop fusion | flops 1572864 | bytes 2097152 | tf_op jit(solution)/shard_map/transpose | solution.py:489
  7.8 0.0 copy-done.2
  7.8 0.1 stack.47
  7.9 0.0 copy-done.3
  7.9 0.1 stack.48
  8.0 1.3 copy_bitcast_fusion.1.r_ref
  9.3 55.6 %gather_tokens.1 = (bf16[1536,512]{1,0:T(8,128)(2,1)}, bf16[64,4,2,2,512]{4,3,2,1,0:T(2,128)(2,1)}) custom-call(bf16[2,96,128]{2,1,0:T(8,128)(2,1)} %bitcast.37, bf16[64,4,2,2,512]{4,3,2,1,0:T(2,128)(2,1)} %copy_bitcast_fusion.r_ref), custom_call_target="tpu_custom_call" | custom-call | tf_op jit(solution)/shard_map/gather_tokens/pallas_call | solution.py:171
  64.9 1.9 %fusion = (bf16[1,64,2,2,512]{4,3,2,0,1:T(2,128)(2,1)S(1)}, bf16[1,64,2,2,512]{4,3,2,0,1:T(2,128)(2,1)S(1)}, bf16[1,64,2,2,512]{4,3,2,0,1:T(2,128)(2,1)S(1)}, bf16[1,64,2,2,512]{4,3,2,0,1:T(2,128)(2,1)S(1)}) fusion(bf16[4,64,2,2,512]{4,3,2,0,1:T(2,128)(2,1)} %bitcast.29), kind=kLoop, calls=%fused_computation.15 | loop fusion | bytes 2097152 | tf_op jit(solution)/shard_map/slice | solution.py:502
  66.9 0.1 stack.42
  67.0 1.1 gather_fusion.1
  68.1 0.1 stack.45
  68.2 1.1 gather_fusion
  69.4 0.1 stack.44
  69.5 0.1 stack.43
  69.6 1.1 pad_maximum_fusion.1
  70.7 54.8 %hidden.1 = (bf16[8,32,1536]{2,1,0:T(8,128)(2,1)}, bf16[64,2,2,2,512]{4,3,2,1,0:T(2,128)(2,1)}) custom-call(bf16[1536,512]{1,0:T(8,128)(2,1)} %get-tuple-element.9.x_ref, bf16[8,128,512]{2,1,0:T(8,128)(2,1)} %bitcast.26, bf16[64,2,2,2,512]{4,3,2,1,0:T(2,128)(2,1)} %copy_bitcast_fusion.1.r_ref), custom_call_target="tpu_custom_call" | custom-call | tf_op jit(solution)/shard_map/hidden/pallas_call | solution.py:354
  125.5 0.0 copy-start
  125.5 2.3 %copy.24 = bf16[256,1536]{0,1:T(8,128)(2,1)} copy(bf16[256,1536]{1,0:T(8,128)(2,1)} %bitcast.34) | data formatting | bytes 1572864 | tf_op jit(solution)/shard_map/reshape | solution.py:505
  127.9 0.0 copy-done
  127.9 0.4 fusion.1
  128.2 1.1 gather_fusion.2
  129.4 0.1 reshape.63
  129.4 0.4 reshape.62
  129.8 0.1 multiply_convert_fusion
  129.9 0.7 broadcast_select_fusion
  130.6 40.6 %merge.1 = bf16[2,96,128]{2,1,0:T(8,128)(2,1)} custom-call(bf16[4,384,256]{2,1,0:T(8,128)(2,1)} %bitcast.27, bf16[256,256]{1,0:T(8,128)(2,1)} %get-tuple-element.20.own_w, bf16[256,256]{1,0:T(8,128)(2,1)} %get-tuple-element.19.other_w), custom_call_target="tpu_custom_call" | custom-call | tf_op jit(solution)/shard_map/merge/pallas_call | solution.py:461
  171.3 1.0 fusion.2
  172.2 0.1 copy.30
  172.3 0.1 copy.29
  172.4 0.6 broadcast_select_fusion.2
Async XLA Ops:
  0.0 5.5 %copy-start.1 = (bf16[256,512]{1,0:T(8,128)(2,1)S(1)}, bf16[256,512]{1,0:T(8,128)(2,1)}, u32[]{:S(2)}) copy-start(bf16[256,512]{1,0:T(8,128)(2,1)} %param.12) | copy-start | bytes 786436
  4.4 3.4 %copy-start.2 = (bf16[256,512]{1,0:T(8,128)(2,1)S(1)}, bf16[256,512]{1,0:T(8,128)(2,1)}, u32[]{:S(2)}) copy-start(bf16[256,512]{1,0:T(8,128)(2,1)} %param.13) | copy-start | bytes 786436
  5.5 2.4 %copy-start.3 = (bf16[256,512]{1,0:T(8,128)(2,1)S(1)}, bf16[256,512]{1,0:T(8,128)(2,1)}, u32[]{:S(2)}) copy-start(bf16[256,512]{1,0:T(8,128)(2,1)} %param.14) | copy-start | bytes 786436
  125.5 2.4 %copy-start = (bf16[64,2,2,2,512]{4,3,2,1,0:T(2,128)(2,1)S(1)}, bf16[64,2,2,2,512]{4,3,2,1,0:T(2,128)(2,1)}, u32[]{:S(2)}) copy-start(bf16[64,2,2,2,512]{4,3,2,1,0:T(2,128)(2,1)} %get-tuple-element.12) | copy-start | bytes 1572868

commit v5 on v4

--- a/solution.py
+++ b/solution.py
@@ -193,7 +193,7 @@
     return v / (1.0 + jnp.exp(-v))
 
 
-def ring_sum(x_ref, w_ref, got, sent, acc, send, recv, z, w, toward, beside):
+def ring_sum(x_ref, w_ref, got, sent, acc, send, recv, z, w, toward, beside, use):
     def product(owner, g):
         return lax.dot_general(
             w_ref[owner],
@@ -252,7 +252,7 @@
     def _(g):
         hop(0, 3, g).wait_recv()
         hop(1, 3, g).wait_recv()
-        acc[g] = acc[g] + got[0, 3, g].astype(F32) + got[1, 3, g].astype(F32)
+        use(g, acc[g] + got[0, 3, g].astype(F32) + got[1, 3, g].astype(F32))
 
     def finish():
         @pl.loop(0, 2)
@@ -294,14 +294,13 @@
         bounds = (1, 17, 33, 49, 64)
         deal_start(r_ref, dealt, d_send, d_recv, z, w, bounds[step], bounds[step + 1])
 
-    finish = ring_sum(x_ref, w_ref, got, sent, acc, send, recv, z, w, toward, beside)
-
-    @pl.loop(0, 4)
-    def _(g):
-        gate_a, up_a, gate_b, up_b = (acc[g, 32 * i : 32 * i + 32] for i in range(4))
+    def activate(g, total):
+        gate_a, up_a, gate_b, up_b = (total[32 * i : 32 * i + 32] for i in range(4))
         hid[0, g] = silu(gate_a) * up_a
         hid[1, g] = silu(gate_b) * up_b
         hid[2, g] = silu(0.5 * (gate_a + gate_b)) * (0.5 * (up_a + up_b))
+
+    finish = ring_sum(x_ref, w_ref, got, sent, acc, send, recv, z, w, toward, beside, activate)
 
     def stats(i):
         center = sum(jnp.sum(hid[i, g], axis=1, keepdims=True) for g in range(GROUPS)) / 1536.0
@@ -321,20 +320,20 @@
 
     def lap(d, s, h):
         slot = (z + 8 - s) % 8 if d == 0 else (z + s) % 8
-        spot = out_ref.at[slot, :, pl.ds(768 * h, 768)]
+        spot = out_ref.at[slot, :, pl.ds(384 * h, 384)]
         return copy_to(spot, spot, ag_send.at[d, s, h], ag_recv.at[d, s, h], toward[d], w)
 
     def arrived(d, s, h):
         slot = (z + 7 - s) % 8 if d == 0 else (z + 1 + s) % 8
-        spot = out_ref.at[slot, :, pl.ds(768 * h, 768)]
+        spot = out_ref.at[slot, :, pl.ds(384 * h, 384)]
         copy_to(spot, spot, ag_send.at[d, s, h], ag_recv.at[d, s, h], toward[d], w).wait_recv()
 
     laps = []
     for s in range(4):
-        for i in range(2):
+        for i in range(4):
             for d in range(2):
-                h = i if d == 0 else 1 - i
-                if s == 3 and i == 1:
+                h = i if d == 0 else (i + 2) % 4
+                if s == 3 and i > 1:
                     continue
                 if s > 0:
                     arrived(d, s - 1, h)
@@ -342,8 +341,9 @@
                 one.start()
                 laps.append(one)
     for d in range(2):
-        arrived(d, 3, d)
-        arrived(d, 2, 1 - d)
+        for i in range(2):
+            arrived(d, 3, 2 * d + i)
+            arrived(d, 2, 2 * (1 - d) + i)
     for one in laps:
         one.wait_send()
     finish()
@@ -360,8 +360,8 @@
         + [
             pltpu.VMEM((GROUPS, 128, 384), F32),
             pltpu.VMEM((3, GROUPS, 32, 384), F32),
-            pltpu.SemaphoreType.DMA((2, 4, 2)),
-            pltpu.SemaphoreType.DMA((2, 4, 2)),
+            pltpu.SemaphoreType.DMA((2, 4, GROUPS)),
+            pltpu.SemaphoreType.DMA((2, 4, GROUPS)),
             pltpu.SemaphoreType.DMA((64,)),
             pltpu.SemaphoreType.DMA((64,)),
         ],
@@ -373,7 +373,7 @@
 
 
 def merge_kernel(
-    h_ref, own_w, other_w, out_ref, own_ref, other_ref, c_got, far_sent, far_got, near_sent, near_got, y_own, y_got, final, send, recv
+    h_ref, own_w, other_w, out_ref, own_ref, other_ref, c_got, far_sent, far_got, near_sent, near_got, y_own, y_sent, y_got, final, send, recv, y_send, y_recv
 ):
     z, w, x, y, c = position()
     q, m = piece_of(x, y, c)
@@ -434,19 +434,35 @@
             for d in range(2):
                 part = part + near_got[d, r // 2, inner, lanes].astype(F32)
             y_own[2 * r + l] = part
-    for k in (4, 3, 5, 2, 6, 1, 7):
-        at = (y + k) % 8
-        move = copy_to(
-            y_own.at[at], y_got.at[k - 1], send.at[9 + k], recv.at[9 + k], z, 16 * x + 2 * at + c
+
+    def y_hop(d, step, p):
+        to = (y + 1 + 6 * d) % 8
+        return copy_to(
+            y_sent.at[d, step, p], y_got.at[d, step, p], y_send.at[d, step, p], y_recv.at[d, step, p],
+            z, 16 * x + 2 * to + c,
         )
-        move.start()
-        moves.append(move)
-    for move in moves[6:]:
-        move.wait_recv()
-    part = y_own[y]
-    for k in range(7):
-        part = part + y_got[k]
-    final[...] = part.astype(BF16)
+
+    for step in range(4):
+        for far in (False, True):
+            for d in range(2):
+                p = d if far else 1 - d
+                if step == 0 and not far:
+                    continue
+                owner = (y + 4 - step) % 8 if d == 0 else (y + 4 + step) % 8
+                value = y_own[owner, 48 * p : 48 * p + 48]
+                if step > (0 if far else 1):
+                    y_hop(d, step - 1, p).wait_recv()
+                    value = value + y_got[d, step - 1, p]
+                y_sent[d, step, p] = value
+                move = y_hop(d, step, p)
+                move.start()
+                moves.append(move)
+    for p in range(2):
+        part = y_own[y, 48 * p : 48 * p + 48]
+        for d in range(2):
+            y_hop(d, 3, p).wait_recv()
+            part = part + y_got[d, 3, p]
+        final[48 * p : 48 * p + 48] = part.astype(BF16)
     for s in range(2):
         either_start(final, out_ref.at[h], send.at[17 + s], recv.at[17 + h], z, w, *targets[s])
     for i in range(2):
@@ -472,10 +488,13 @@
             pltpu.VMEM((2, 2, 192, 256), BF16),
             pltpu.VMEM((2, 2, 192, 256), BF16),
             pltpu.VMEM((8, 96, 128), F32),
-            pltpu.VMEM((7, 96, 128), F32),
+            pltpu.VMEM((2, 4, 2, 48, 128), F32),
+            pltpu.VMEM((2, 4, 2, 48, 128), F32),
             pltpu.VMEM((96, 128), BF16),
             pltpu.SemaphoreType.DMA((19,)),
             pltpu.SemaphoreType.DMA((19,)),
+            pltpu.SemaphoreType.DMA((2, 4, 2)),
+            pltpu.SemaphoreType.DMA((2, 4, 2)),
         ],
         compiler_params=pltpu.CompilerParams(
             collective_id=2, has_side_effects=True, vmem_limit_bytes=VMEM_BYTES

time: 174 us -> 177 us (1.017)
  the two profiles are of different devices: /device:TPU:11 before, /device:TPU:13 now
where the time goes in v5:
time: 177 us; the launch traced here: 176 us
  Pallas kernels  154 us (87%)
  local copies, waits for them, and re-layouts  13.9 us (8%)
  other arithmetic  7.91 us (4%)
    pallas_call x1, Pallas kernels, hidden(): pl.pallas_call(hidden_kernel, out_shape=(jax.ShapeDtypeStruct((8, 32, 153...  54.8 us
    pallas_call x1, Pallas kernels, gather_tokens(): pl.pallas_call(tokens_kernel, out_shape=(jax.ShapeDtypeStruct((1536, 512)...  54.3 us
    pallas_call x1, Pallas kernels, merge(): pl.pallas_call(merge_kernel, out_shape=jax.ShapeDtypeStruct((2, 96, 128),...  45.2 us

profile of v5, /device:TPU:13, one launch (start us, length us, event | category | flops | bytes accessed | tf_op | source)
XLA Modules:
  0.0 176.3 jit_solution(2251939395067264057)
XLA Ops:
  0.0 0.0 copy-start.1
  0.0 0.7 pad_clamp_fusion
  0.7 0.8 pad_select_fusion
  1.6 0.7 copy.15
  2.3 1.1 stack.37
  3.3 1.1 stack.38
  4.4 0.0 copy-start.2
  4.4 1.1 stack.39
  5.5 0.0 copy-done.1
  5.5 0.0 copy-start.3
  5.5 0.1 stack.40
  5.6 2.2 %copy_bitcast_fusion.r_ref = bf16[64,4,2,2,512]{4,3,2,1,0:T(2,128)(2,1)} fusion(bf16[1,2,64,2,512]{4,3,2,1,0:T(2,128)(2,1)S(1)} %stack.40, bf16[1,2,64,2,512]{4,3,2,1,0:T(2,128)(2,1)S(1)} %stack.39, bf16[1,2,64,2,512]{4,3,2,1,0:T(2,128)(2,1)S(1)} %stack.38, bf16[1,2,64,2,512]{4,3,2,1,0:T(2,128)(2,1)S(1)} %stack.37), kind=kLoop, calls=%fused_computation.5 | loop fusion | flops 1572864 | bytes 2097152 | tf_op jit(solution)/shard_map/transpose | solution.py:508
  7.8 0.0 copy-done.2
  7.8 0.1 stack.47
  7.9 0.0 copy-done.3
  7.9 0.1 stack.48
  8.0 1.3 copy_bitcast_fusion.1.r_ref
  9.3 54.3 %gather_tokens.1 = (bf16[1536,512]{1,0:T(8,128)(2,1)}, bf16[64,4,2,2,512]{4,3,2,1,0:T(2,128)(2,1)}) custom-call(bf16[2,96,128]{2,1,0:T(8,128)(2,1)} %bitcast.37, bf16[64,4,2,2,512]{4,3,2,1,0:T(2,128)(2,1)} %copy_bitcast_fusion.r_ref), custom_call_target="tpu_custom_call" | custom-call | tf_op jit(solution)/shard_map/gather_tokens/pallas_call | solution.py:171
  63.7 1.9 %fusion = (bf16[1,64,2,2,512]{4,3,2,0,1:T(2,128)(2,1)S(1)}, bf16[1,64,2,2,512]{4,3,2,0,1:T(2,128)(2,1)S(1)}, bf16[1,64,2,2,512]{4,3,2,0,1:T(2,128)(2,1)S(1)}, bf16[1,64,2,2,512]{4,3,2,0,1:T(2,128)(2,1)S(1)}) fusion(bf16[4,64,2,2,512]{4,3,2,0,1:T(2,128)(2,1)} %bitcast.29), kind=kLoop, calls=%fused_computation.15 | loop fusion | bytes 2097152 | tf_op jit(solution)/shard_map/slice | solution.py:521
  65.6 0.1 stack.42
  65.7 1.1 gather_fusion.1
  66.8 0.1 stack.45
  66.9 1.1 gather_fusion
  68.1 0.1 stack.44
  68.2 0.1 stack.43
  68.3 1.1 pad_maximum_fusion.1
  69.4 54.8 %hidden.1 = (bf16[8,32,1536]{2,1,0:T(8,128)(2,1)}, bf16[64,2,2,2,512]{4,3,2,1,0:T(2,128)(2,1)}) custom-call(bf16[1536,512]{1,0:T(8,128)(2,1)} %get-tuple-element.9.x_ref, bf16[8,128,512]{2,1,0:T(8,128)(2,1)} %bitcast.26, bf16[64,2,2,2,512]{4,3,2,1,0:T(2,128)(2,1)} %copy_bitcast_fusion.1.r_ref), custom_call_target="tpu_custom_call" | custom-call | tf_op jit(solution)/shard_map/hidden/pallas_call | solution.py:354
  124.2 0.0 copy-start
  124.2 2.3 %copy.24 = bf16[256,1536]{0,1:T(8,128)(2,1)} copy(bf16[256,1536]{1,0:T(8,128)(2,1)} %bitcast.34) | data formatting | bytes 1572864 | tf_op jit(solution)/shard_map/reshape | solution.py:524
  126.5 0.0 copy-done
  126.5 0.4 fusion.1
  126.9 1.1 gather_fusion.2
  128.0 0.1 reshape.63
  128.1 0.4 reshape.62
  128.5 0.1 multiply_convert_fusion
  128.6 0.7 broadcast_select_fusion
  129.3 45.2 %merge.1 = bf16[2,96,128]{2,1,0:T(8,128)(2,1)} custom-call(bf16[4,384,256]{2,1,0:T(8,128)(2,1)} %bitcast.27, bf16[256,256]{1,0:T(8,128)(2,1)} %get-tuple-element.20.own_w, bf16[256,256]{1,0:T(8,128)(2,1)} %get-tuple-element.19.other_w), custom_call_target="tpu_custom_call" | custom-call | tf_op jit(solution)/shard_map/merge/pallas_call | solution.py:477
  174.5 1.0 fusion.2
  175.5 0.1 copy.30
  175.6 0.1 copy.29
  175.7 0.6 broadcast_select_fusion.2
Async XLA Ops:
  0.0 5.5 %copy-start.1 = (bf16[256,512]{1,0:T(8,128)(2,1)S(1)}, bf16[256,512]{1,0:T(8,128)(2,1)}, u32[]{:S(2)}) copy-start(bf16[256,512]{1,0:T(8,128)(2,1)} %param.12) | copy-start | bytes 786436
  4.4 3.4 %copy-start.2 = (bf16[256,512]{1,0:T(8,128)(2,1)S(1)}, bf16[256,512]{1,0:T(8,128)(2,1)}, u32[]{:S(2)}) copy-start(bf16[256,512]{1,0:T(8,128)(2,1)} %param.13) | copy-start | bytes 786436
  5.5 2.4 %copy-start.3 = (bf16[256,512]{1,0:T(8,128)(2,1)S(1)}, bf16[256,512]{1,0:T(8,128)(2,1)}, u32[]{:S(2)}) copy-start(bf16[256,512]{1,0:T(8,128)(2,1)} %param.14) | copy-start | bytes 786436
  124.2 2.4 %copy-start = (bf16[64,2,2,2,512]{4,3,2,1,0:T(2,128)(2,1)S(1)}, bf16[64,2,2,2,512]{4,3,2,1,0:T(2,128)(2,1)}, u32[]{:S(2)}) copy-start(bf16[64,2,2,2,512]{4,3,2,1,0:T(2,128)(2,1)} %get-tuple-element.12) | copy-start | bytes 1572868

commit v6 on v4

--- a/solution.py
+++ b/solution.py
@@ -1,5 +1,3 @@
-import functools
-
 import jax
 import jax.numpy as jnp
 from jax import lax
@@ -193,7 +191,7 @@
     return v / (1.0 + jnp.exp(-v))
 
 
-def ring_sum(x_ref, w_ref, got, sent, acc, send, recv, z, w, toward, beside):
+def ring_sum(x_ref, w_ref, got, sent, acc, send, recv, z, w, toward, beside, use):
     def product(owner, g):
         return lax.dot_general(
             w_ref[owner],
@@ -252,7 +250,7 @@
     def _(g):
         hop(0, 3, g).wait_recv()
         hop(1, 3, g).wait_recv()
-        acc[g] = acc[g] + got[0, 3, g].astype(F32) + got[1, 3, g].astype(F32)
+        use(g, acc[g] + got[0, 3, g].astype(F32) + got[1, 3, g].astype(F32))
 
     def finish():
         @pl.loop(0, 2)
@@ -294,14 +292,13 @@
         bounds = (1, 17, 33, 49, 64)
         deal_start(r_ref, dealt, d_send, d_recv, z, w, bounds[step], bounds[step + 1])
 
-    finish = ring_sum(x_ref, w_ref, got, sent, acc, send, recv, z, w, toward, beside)
-
-    @pl.loop(0, 4)
-    def _(g):
-        gate_a, up_a, gate_b, up_b = (acc[g, 32 * i : 32 * i + 32] for i in range(4))
+    def activate(g, total):
+        gate_a, up_a, gate_b, up_b = (total[32 * i : 32 * i + 32] for i in range(4))
         hid[0, g] = silu(gate_a) * up_a
         hid[1, g] = silu(gate_b) * up_b
         hid[2, g] = silu(0.5 * (gate_a + gate_b)) * (0.5 * (up_a + up_b))
+
+    finish = ring_sum(x_ref, w_ref, got, sent, acc, send, recv, z, w, toward, beside, activate)
 
     def stats(i):
         center = sum(jnp.sum(hid[i, g], axis=1, keepdims=True) for g in range(GROUPS)) / 1536.0
@@ -321,20 +318,20 @@
 
     def lap(d, s, h):
         slot = (z + 8 - s) % 8 if d == 0 else (z + s) % 8
-        spot = out_ref.at[slot, :, pl.ds(768 * h, 768)]
+        spot = out_ref.at[slot, :, pl.ds(384 * h, 384)]
         return copy_to(spot, spot, ag_send.at[d, s, h], ag_recv.at[d, s, h], toward[d], w)
 
     def arrived(d, s, h):
         slot = (z + 7 - s) % 8 if d == 0 else (z + 1 + s) % 8
-        spot = out_ref.at[slot, :, pl.ds(768 * h, 768)]
+        spot = out_ref.at[slot, :, pl.ds(384 * h, 384)]
         copy_to(spot, spot, ag_send.at[d, s, h], ag_recv.at[d, s, h], toward[d], w).wait_recv()
 
     laps = []
     for s in range(4):
-        for i in range(2):
+        for i in range(4):
             for d in range(2):
-                h = i if d == 0 else 1 - i
-                if s == 3 and i == 1:
+                h = i if d == 0 else (i + 2) % 4
+                if s == 3 and i > 1:
                     continue
                 if s > 0:
                     arrived(d, s - 1, h)
@@ -342,8 +339,9 @@
                 one.start()
                 laps.append(one)
     for d in range(2):
-        arrived(d, 3, d)
-        arrived(d, 2, 1 - d)
+        for i in range(2):
+            arrived(d, 3, 2 * d + i)
+            arrived(d, 2, 2 * (1 - d) + i)
     for one in laps:
         one.wait_send()
     finish()
@@ -360,8 +358,8 @@
         + [
             pltpu.VMEM((GROUPS, 128, 384), F32),
             pltpu.VMEM((3, GROUPS, 32, 384), F32),
-            pltpu.SemaphoreType.DMA((2, 4, 2)),
-            pltpu.SemaphoreType.DMA((2, 4, 2)),
+            pltpu.SemaphoreType.DMA((2, 4, GROUPS)),
+            pltpu.SemaphoreType.DMA((2, 4, GROUPS)),
             pltpu.SemaphoreType.DMA((64,)),
             pltpu.SemaphoreType.DMA((64,)),
         ],
@@ -496,15 +494,18 @@
 
 def local(tokens, gate_a, up_a, gate_b, up_b, down_a, down_b, block_perm):
     c = lax.axis_index("wid") % 2
-    take = functools.partial(jnp.take, indices=block_perm, mode="clip")
+
+    def take(blocks):
+        return blocks.at[block_perm].get(mode="promise_in_bounds")
+
     x, rows = gather_tokens(tokens, by_dest(gate_a, up_a, gate_b, up_b))
     rows = by_block(rows)
-    weights = jnp.stack((rows[0], rows[1], take(rows[2], axis=0), take(rows[3], axis=0)))
+    weights = jnp.stack((rows[0], rows[1], take(rows[2]), take(rows[3])))
     weights = weights.reshape(4, 8, 32, 512).transpose(1, 0, 2, 3).reshape(8, 128, 512)
     repaired, rows = hidden(x, weights, by_dest(down_a, down_b))
     repaired = repaired.reshape(256, 1536)
     rows = by_block(rows)
-    down_mid = ((rows[0].astype(F32) + take(rows[1], axis=0).astype(F32)) * 0.5).astype(BF16).reshape(256, 512)
+    down_mid = ((rows[0].astype(F32) + take(rows[1]).astype(F32)) * 0.5).astype(BF16).reshape(256, 512)
 
     halves = (down_mid[:, :256], down_mid[:, 256:])
     own = jnp.where(c == 0, *halves)

time: 174 us -> 174 us (level)
  the two profiles are of different devices: /device:TPU:11 before, /device:TPU:3 now
where the time goes in v6:
time: 174 us
  Pallas kernels  152 us (87%)
  local copies, waits for them, and re-layouts  13.9 us (8%)
  other arithmetic  7.92 us (5%)
    pallas_call x1, Pallas kernels, hidden(): pl.pallas_call(hidden_kernel, out_shape=(jax.ShapeDtypeStruct((8, 32, 153...  55.4 us
    pallas_call x1, Pallas kernels, gather_tokens(): pl.pallas_call(tokens_kernel, out_shape=(jax.ShapeDtypeStruct((1536, 512)...  54.7 us
    pallas_call x1, Pallas kernels, merge(): pl.pallas_call(merge_kernel, out_shape=jax.ShapeDtypeStruct((2, 96, 128),...  41.6 us
    another operation x6, local copies, waits for them, and re-layouts, by_dest(): jnp.stack(matrices).reshape(n, 2, 64, 2, 512).transpose(2, 0, 1, 3, 4)  3.51 us

profile of v6, /device:TPU:3, one launch (start us, length us, event | category | flops | bytes accessed | tf_op | source)
XLA Modules:
  0.0 173.7 jit_solution(5830903830439710556)
XLA Ops:
  0.0 0.0 copy-start.1
  0.0 0.7 compare_select_fusion
  0.7 0.8 pad_select_fusion
  1.6 0.7 copy.15
  2.3 1.1 stack.37
  3.3 1.1 stack.38
  4.4 0.0 copy-start.2
  4.4 1.1 stack.39
  5.5 0.0 copy-done.1
  5.5 0.0 copy-start.3
  5.5 0.1 stack.40
  5.6 2.2 %copy_bitcast_fusion.r_ref = bf16[64,4,2,2,512]{4,3,2,1,0:T(2,128)(2,1)} fusion(bf16[1,2,64,2,512]{4,3,2,1,0:T(2,128)(2,1)S(1)} %stack.40, bf16[1,2,64,2,512]{4,3,2,1,0:T(2,128)(2,1)S(1)} %stack.39, bf16[1,2,64,2,512]{4,3,2,1,0:T(2,128)(2,1)S(1)} %stack.38, bf16[1,2,64,2,512]{4,3,2,1,0:T(2,128)(2,1)S(1)} %stack.37), kind=kLoop, calls=%fused_computation.5 | loop fusion | flops 1572864 | bytes 2097152 | tf_op jit(solution)/shard_map/transpose | solution.py:487
  7.8 0.0 copy-done.2
  7.8 0.1 stack.47
  7.9 0.0 copy-done.3
  7.9 0.1 stack.48
  8.0 1.3 copy_bitcast_fusion.1.r_ref
  9.3 54.7 %gather_tokens.1 = (bf16[1536,512]{1,0:T(8,128)(2,1)}, bf16[64,4,2,2,512]{4,3,2,1,0:T(2,128)(2,1)}) custom-call(bf16[2,96,128]{2,1,0:T(8,128)(2,1)} %bitcast.37, bf16[64,4,2,2,512]{4,3,2,1,0:T(2,128)(2,1)} %copy_bitcast_fusion.r_ref), custom_call_target="tpu_custom_call" | custom-call | tf_op jit(solution)/shard_map/gather_tokens/pallas_call | solution.py:169
  64.0 1.9 %fusion = (bf16[1,64,2,2,512]{4,3,2,0,1:T(2,128)(2,1)S(1)}, bf16[1,64,2,2,512]{4,3,2,0,1:T(2,128)(2,1)S(1)}, bf16[1,64,2,2,512]{4,3,2,0,1:T(2,128)(2,1)S(1)}, bf16[1,64,2,2,512]{4,3,2,0,1:T(2,128)(2,1)S(1)}) fusion(bf16[4,64,2,2,512]{4,3,2,0,1:T(2,128)(2,1)} %bitcast.29), kind=kLoop, calls=%fused_computation.16 | loop fusion | bytes 2097152 | tf_op jit(solution)/shard_map/slice | solution.py:503
  66.0 0.1 stack.42
  66.1 1.1 gather_fusion.1
  67.2 0.1 stack.45
  67.3 1.1 gather_fusion
  68.4 0.1 stack.44
  68.5 0.1 stack.43
  68.7 1.1 pad_maximum_fusion.1
  69.8 55.4 %hidden.1 = (bf16[8,32,1536]{2,1,0:T(8,128)(2,1)}, bf16[64,2,2,2,512]{4,3,2,1,0:T(2,128)(2,1)}) custom-call(bf16[1536,512]{1,0:T(8,128)(2,1)} %get-tuple-element.9.x_ref, bf16[8,128,512]{2,1,0:T(8,128)(2,1)} %bitcast.26, bf16[64,2,2,2,512]{4,3,2,1,0:T(2,128)(2,1)} %copy_bitcast_fusion.1.r_ref), custom_call_target="tpu_custom_call" | custom-call | tf_op jit(solution)/shard_map/hidden/pallas_call | solution.py:352
  125.1 0.0 copy-start
  125.2 2.3 %copy.24 = bf16[256,1536]{0,1:T(8,128)(2,1)} copy(bf16[256,1536]{1,0:T(8,128)(2,1)} %bitcast.34) | data formatting | bytes 1572864 | tf_op jit(solution)/shard_map/reshape | solution.py:506
  127.5 0.0 copy-done
  127.5 0.4 fusion.1
  127.9 1.1 gather_fusion.2
  129.0 0.1 reshape.63
  129.1 0.4 reshape.62
  129.5 0.1 multiply_convert_fusion
  129.6 0.7 broadcast_select_fusion
  130.3 41.6 %merge.1 = bf16[2,96,128]{2,1,0:T(8,128)(2,1)} custom-call(bf16[4,384,256]{2,1,0:T(8,128)(2,1)} %bitcast.27, bf16[256,256]{1,0:T(8,128)(2,1)} %get-tuple-element.20.own_w, bf16[256,256]{1,0:T(8,128)(2,1)} %get-tuple-element.19.other_w), custom_call_target="tpu_custom_call" | custom-call | tf_op jit(solution)/shard_map/merge/pallas_call | solution.py:459
  171.9 1.0 fusion.2
  172.9 0.1 copy.30
  173.0 0.1 copy.29
  173.1 0.6 broadcast_select_fusion.2
  (1 shorter events, 0.0 us)
Async XLA Ops:
  0.0 5.5 %copy-start.1 = (bf16[256,512]{1,0:T(8,128)(2,1)S(1)}, bf16[256,512]{1,0:T(8,128)(2,1)}, u32[]{:S(2)}) copy-start(bf16[256,512]{1,0:T(8,128)(2,1)} %param.12) | copy-start | bytes 786436
  4.4 3.4 %copy-start.2 = (bf16[256,512]{1,0:T(8,128)(2,1)S(1)}, bf16[256,512]{1,0:T(8,128)(2,1)}, u32[]{:S(2)}) copy-start(bf16[256,512]{1,0:T(8,128)(2,1)} %param.13) | copy-start | bytes 786436
  5.5 2.4 %copy-start.3 = (bf16[256,512]{1,0:T(8,128)(2,1)S(1)}, bf16[256,512]{1,0:T(8,128)(2,1)}, u32[]{:S(2)}) copy-start(bf16[256,512]{1,0:T(8,128)(2,1)} %param.14) | copy-start | bytes 786436
  125.1 2.4 %copy-start = (bf16[64,2,2,2,512]{4,3,2,1,0:T(2,128)(2,1)S(1)}, bf16[64,2,2,2,512]{4,3,2,1,0:T(2,128)(2,1)}, u32[]{:S(2)}) copy-start(bf16[64,2,2,2,512]{4,3,2,1,0:T(2,128)(2,1)} %get-tuple-element.12) | copy-start | bytes 1572868
